TPU v7x, 128 devices: a whole 4x4x4 slice. The times are simulated.
128 devices in a mesh: gx: 16 (over z_hi, x, core), gy: 8 (over z_lo, y).
Axes of the slice: x: 4, y: 4, z: 4 (z_hi: 2, z_lo: 2; z = z_hi * 2 + z_lo), core: 2. Of those that a mesh axis runs over, the one named last changes fastest.
Arguments:
- multipoles: float32 [10, 1048576], P(None, ('gx', 'gy')), may hold values from -8 to 8
- fractions: float32 [3, 1048576], P(None, ('gx', 'gy')), may hold values from 0 to 1
- base_index: int32 [3, 1048576], P(None, ('gx', 'gy')), may hold values from 0 to 252, as said below
- block_plane: int32 [8192], P(('gx', 'gy')), may hold values from 0 to 3
- atom_count: int32 [8192], P(('gx', 'gy')), may hold values from 32 to 128, as said below
- coupling: float32 [8, 256, 256], replicated, may hold values from -0.375 to 0.375
Outputs:
- coupled: float32 [2, 256, 512, 256], P(None, ('gx', 'gy'))
Inputs may be any that keep to these rules, and one draw needn't show every extreme that they name: `base_index`: row 0 is an atom's x cell within its block's plane block, 0 to 7; row 1 its y cell within its device's 64 columns, 0 to 63; row 2 its z cell, 0 to 252. Atoms of the slots of device d lie in device d's cells. `atom_count`: slots of a block at or past its count are padding whose values are to be ignored.
All inputs are finite; a program needn't handle non-finite values.
Results may differ from a plain program's by a relative error of at most 0.0042.
Values sent between devices are 32-bit elements; how exact they have to be, the bound alone decides.
No kernel may reach another device: no remote copies, remote signals or barrier semaphores. Data moves between devices by JAX's collectives and lax.ppermute only.
A program may use at most 64 MiB of HBM per device.

v0:
```python
import math

import jax
import jax.numpy as jnp
from jax import lax
from jax.sharding import PartitionSpec as P

NX = 512
NY = 512
NZ = 256
XB = 8
SLOT_BLK = 128
MBLK = 8
KX = 256


def from_behind(value, axis, by):
    devices = lax.axis_size(axis)
    return lax.ppermute(value, axis, [(i, (i + by) % devices) for i in range(devices)])


def spline_weights(fraction):
    remain = 1.0 - fraction
    square = fraction * fraction
    cubed = square * fraction
    values = jnp.stack(
        [
            remain * remain * remain / 6.0,
            (3.0 * cubed - 6.0 * square + 4.0) / 6.0,
            (-3.0 * cubed + 3.0 * square + 3.0 * fraction + 1.0) / 6.0,
            cubed / 6.0,
        ]
    )
    slopes = jnp.stack(
        [
            -remain * remain / 2.0,
            (3.0 * square - 4.0 * fraction) / 2.0,
            (-3.0 * square + 2.0 * fraction + 1.0) / 2.0,
            square / 2.0,
        ]
    )
    curves = jnp.stack([remain, 3.0 * fraction - 2.0, 1.0 - 3.0 * fraction, fraction])
    return jnp.stack([values, slopes, curves])


def plane_weights(moments, spline_x, spline_y):
    x_spline = spline_x[:, :, None]
    y_spline = spline_y[:, None, :]
    moment = moments[:, None, None]
    order_zero = (
        moment[0] * x_spline[0] * y_spline[0]
        + moment[1] * x_spline[1] * y_spline[0]
        + moment[2] * x_spline[0] * y_spline[1]
        + moment[4] * x_spline[2] * y_spline[0]
        + moment[5] * x_spline[0] * y_spline[2]
        + moment[7] * x_spline[1] * y_spline[1]
    )
    order_one = (
        moment[3] * x_spline[0] * y_spline[0]
        + moment[8] * x_spline[1] * y_spline[0]
        + moment[9] * x_spline[0] * y_spline[1]
    )
    order_two = moment[6] * x_spline[0] * y_spline[0]
    return jnp.stack([order_zero, order_one, order_two]).astype(jnp.bfloat16)


def selector(positions, width, tap_ids):
    window_ids = jnp.arange(width, dtype=jnp.int32)
    hits = window_ids[None, :, None, None] == positions[None, None] + tap_ids[:, None, None, None]
    return hits.astype(jnp.bfloat16)


def per_device(multipoles, fractions, base_index, block_plane, atom_count, coupling):
    cells_x = NX // lax.axis_size("gx")
    cells_y = NY // lax.axis_size("gy")
    block_count = block_plane.shape[0]
    slot_rank = jnp.arange(SLOT_BLK, dtype=jnp.int32)
    live_slot = (slot_rank[None, :] < atom_count[:, None]).astype(jnp.float32)
    moments = multipoles.reshape(10, block_count, SLOT_BLK) * live_slot[None]
    fraction = fractions.reshape(3, block_count, SLOT_BLK)
    cell_rows = base_index.reshape(3, block_count, SLOT_BLK)
    planes = plane_weights(moments, spline_weights(fraction[0]), spline_weights(fraction[1]))
    z_weights = spline_weights(fraction[2]).astype(jnp.bfloat16)
    width_x = XB + 3
    width_y = cells_y + 3
    tap_ids = jnp.arange(4, dtype=jnp.int32)
    per_turn = 4

    def spread_turn(turn, extended):
        first_block = turn * per_turn
        plane_part = lax.dynamic_slice_in_dim(planes, first_block, per_turn, 3)
        zweight_part = lax.dynamic_slice_in_dim(z_weights, first_block, per_turn, 2)
        cell_part = lax.dynamic_slice_in_dim(cell_rows, first_block, per_turn, 1)
        x_select = selector(cell_part[0], width_x, tap_ids)
        y_select = selector(cell_part[1], width_y, tap_ids)
        z_select = selector(cell_part[2], NZ, tap_ids)
        rows_y = jnp.einsum(
            "kabgs,bygs->kaygs", plane_part, y_select, preferred_element_type=jnp.float32
        ).astype(jnp.bfloat16)
        window = jnp.einsum(
            "axgs,kaygs->gkxys", x_select, rows_y, preferred_element_type=jnp.float32
        ).astype(jnp.bfloat16)
        z_window = jnp.einsum(
            "kcgs,czgs->gksz", zweight_part, z_select, preferred_element_type=jnp.float32
        ).astype(jnp.bfloat16)
        pieces = jnp.einsum(
            "gkxys,gksz->gxyz", window, z_window, preferred_element_type=jnp.float32
        )
        for member in range(per_turn):
            plane_start = block_plane[first_block + member] * XB
            current = lax.dynamic_slice(extended, (plane_start, 0, 0), (width_x, width_y, NZ))
            extended = lax.dynamic_update_slice(
                extended, current + pieces[member], (plane_start, 0, 0)
            )
        return extended

    extended = lax.fori_loop(
        0, block_count // per_turn, spread_turn, jnp.zeros((cells_x + 3, width_y, NZ), jnp.float32)
    )
    rim_x = from_behind(extended[cells_x:], "gx", 1)
    density = extended[:cells_x].at[:3].add(rim_x)
    rim_y = from_behind(density[:, cells_y:], "gy", 1)
    density = density[:, :cells_y].at[:, :3].add(rim_y)
    wave_x = jnp.arange(KX, dtype=jnp.int32)[:, None]
    cell_x = jnp.arange(NX, dtype=jnp.int32)[None, :]
    phase_x = (wave_x * cell_x % NX).astype(jnp.float32) * (2.0 * math.pi / NX)
    scale = 1.0 / math.sqrt(NX * NY)
    table_x = jnp.concatenate([jnp.cos(phase_x) * scale, -jnp.sin(phase_x) * scale], 0)
    lines = lax.all_to_all(density, "gx", split_axis=1, concat_axis=0, tiled=True)
    result = jnp.einsum("kx,xyz->kyz", table_x, lines, precision=lax.Precision.HIGHEST)
    spectrum = result.reshape(2, KX, lines.shape[1], lines.shape[2])
    spectrum = lax.all_to_all(
        lax.all_to_all(spectrum, "gx", split_axis=1, concat_axis=2, tiled=True),
        "gy",
        split_axis=1,
        concat_axis=2,
        tiled=True,
    )
    y_order = jnp.arange(NY, dtype=jnp.int32)
    wave_y = jnp.arange(NY, dtype=jnp.int32)[:, None]
    phase_y = (wave_y * y_order[None, :] % NY).astype(jnp.float32) * (2.0 * math.pi / NY)
    cosine_part = jnp.einsum(
        "qr,ckrz->ckqz", jnp.cos(phase_y), spectrum, precision=lax.Precision.HIGHEST
    )
    sine_part = jnp.einsum(
        "qr,ckrz->ckqz", jnp.sin(phase_y), spectrum, precision=lax.Precision.HIGHEST
    )
    real_part = cosine_part[0] + sine_part[1]
    imag_part = cosine_part[1] - sine_part[0]
    mode_rows = real_part.shape[0]
    stacked = jnp.stack([real_part, imag_part]).reshape(2, mode_rows, MBLK, NY // MBLK, NZ)
    coupled = jnp.einsum("ckbjw,bzw->ckbjz", stacked, coupling, precision=lax.Precision.HIGHEST)
    return coupled.reshape(2, mode_rows, NY, NZ)


def solution(mesh):
    return jax.shard_map(
        per_device,
        mesh=mesh,
        in_specs=(
            P(None, ("gx", "gy")),
            P(None, ("gx", "gy")),
            P(None, ("gx", "gy")),
            P(("gx", "gy")),
            P(("gx", "gy")),
            P(),
        ),
        out_specs=P(None, ("gx", "gy"), None, None),
        check_vma=False,
    )
```

profile of v0, /device:TPU:1, one launch (start us, length us, event | category | flops | bytes accessed | tf_op | source)
XLA Modules:
  0.0 689.3 jit_solution(6725854517000739928)
XLA Ops:
  6.6 517.3 %while.19 = (s32[]{:T(128)}, f32[35,67,256]{2,1,0:T(8,128)}, s32[64]{0:T(128)S(1)}, s32[3,64,128]{2,1,0:T(8,128)S(1)}, bf16[3,4,4,64,128]{4,3,2,1,0:T(8,128)(2,1...) while((s32[]{:T(128)}, f32[35,67,256]{2,1,0:T(8,128)}, ...), condition=%wide.region_1.0_spmd.clone.clone, body=%wide.region_0.0_spmd.clone.clone.sunk | while | flops 598477312 | bytes 19227272 | solution.py:117
  10.2 8.0 %convert_bitcast_fusion.2 = bf16[4,3,11,67,128]{3,2,1,4,0:T(8,128)(2,1)} fusion(bf16[3,4,4,4,128]{2,1,0,4,3:T(4,128)(2,1)} %copy.128, s32[4,4,128]{0,2,1:T(8,128)S(1)} %get-tuple-element.395, s32[4,4,128]{0,2,1:T(8,128)S(1)} %iota_add_fusion.6), kind=kOutput, calls=%fused_computation.1.clone.1 | convolution fusion | flops 14052864 | bytes 2329600 | tf_op jit(solution)/shard_map/while/body/eval_jaxpr/axgs,kaygs->gkxys/dot_general | solution.py:100
  20.2 6.0 fusion.138
  42.5 8.0 %convert_bitcast_fusion.2 = bf16[4,3,11,67,128]{3,2,1,4,0:T(8,128)(2,1)} fusion(bf16[3,4,4,4,128]{2,1,0,4,3:T(4,128)(2,1)} %copy.128, s32[4,4,128]{0,2,1:T(8,128)S(1)} %get-tuple-element.395, s32[4,4,128]{0,2,1:T(8,128)S(1)} %iota_add_fusion.6), kind=kOutput, calls=%fused_computation.1.clone.1 | convolution fusion | flops 14052864 | bytes 2329600 | tf_op jit(solution)/shard_map/while/body/eval_jaxpr/axgs,kaygs->gkxys/dot_general | solution.py:100
  74.8 8.0 %convert_bitcast_fusion.2 = bf16[4,3,11,67,128]{3,2,1,4,0:T(8,128)(2,1)} fusion(bf16[3,4,4,4,128]{2,1,0,4,3:T(4,128)(2,1)} %copy.128, s32[4,4,128]{0,2,1:T(8,128)S(1)} %get-tuple-element.395, s32[4,4,128]{0,2,1:T(8,128)S(1)} %iota_add_fusion.6), kind=kOutput, calls=%fused_computation.1.clone.1 | convolution fusion | flops 14052864 | bytes 2329600 | tf_op jit(solution)/shard_map/while/body/eval_jaxpr/axgs,kaygs->gkxys/dot_general | solution.py:100
  107.2 8.0 %convert_bitcast_fusion.2 = bf16[4,3,11,67,128]{3,2,1,4,0:T(8,128)(2,1)} fusion(bf16[3,4,4,4,128]{2,1,0,4,3:T(4,128)(2,1)} %copy.128, s32[4,4,128]{0,2,1:T(8,128)S(1)} %get-tuple-element.395, s32[4,4,128]{0,2,1:T(8,128)S(1)} %iota_add_fusion.6), kind=kOutput, calls=%fused_computation.1.clone.1 | convolution fusion | flops 14052864 | bytes 2329600 | tf_op jit(solution)/shard_map/while/body/eval_jaxpr/axgs,kaygs->gkxys/dot_general | solution.py:100
  139.5 8.0 %convert_bitcast_fusion.2 = bf16[4,3,11,67,128]{3,2,1,4,0:T(8,128)(2,1)} fusion(bf16[3,4,4,4,128]{2,1,0,4,3:T(4,128)(2,1)} %copy.128, s32[4,4,128]{0,2,1:T(8,128)S(1)} %get-tuple-element.395, s32[4,4,128]{0,2,1:T(8,128)S(1)} %iota_add_fusion.6), kind=kOutput, calls=%fused_computation.1.clone.1 | convolution fusion | flops 14052864 | bytes 2329600 | tf_op jit(solution)/shard_map/while/body/eval_jaxpr/axgs,kaygs->gkxys/dot_general | solution.py:100
  171.8 8.0 %convert_bitcast_fusion.2 = bf16[4,3,11,67,128]{3,2,1,4,0:T(8,128)(2,1)} fusion(bf16[3,4,4,4,128]{2,1,0,4,3:T(4,128)(2,1)} %copy.128, s32[4,4,128]{0,2,1:T(8,128)S(1)} %get-tuple-element.395, s32[4,4,128]{0,2,1:T(8,128)S(1)} %iota_add_fusion.6), kind=kOutput, calls=%fused_computation.1.clone.1 | convolution fusion | flops 14052864 | bytes 2329600 | tf_op jit(solution)/shard_map/while/body/eval_jaxpr/axgs,kaygs->gkxys/dot_general | solution.py:100
  204.2 8.0 %convert_bitcast_fusion.2 = bf16[4,3,11,67,128]{3,2,1,4,0:T(8,128)(2,1)} fusion(bf16[3,4,4,4,128]{2,1,0,4,3:T(4,128)(2,1)} %copy.128, s32[4,4,128]{0,2,1:T(8,128)S(1)} %get-tuple-element.395, s32[4,4,128]{0,2,1:T(8,128)S(1)} %iota_add_fusion.6), kind=kOutput, calls=%fused_computation.1.clone.1 | convolution fusion | flops 14052864 | bytes 2329600 | tf_op jit(solution)/shard_map/while/body/eval_jaxpr/axgs,kaygs->gkxys/dot_general | solution.py:100
  236.5 8.0 %convert_bitcast_fusion.2 = bf16[4,3,11,67,128]{3,2,1,4,0:T(8,128)(2,1)} fusion(bf16[3,4,4,4,128]{2,1,0,4,3:T(4,128)(2,1)} %copy.128, s32[4,4,128]{0,2,1:T(8,128)S(1)} %get-tuple-element.395, s32[4,4,128]{0,2,1:T(8,128)S(1)} %iota_add_fusion.6), kind=kOutput, calls=%fused_computation.1.clone.1 | convolution fusion | flops 14052864 | bytes 2329600 | tf_op jit(solution)/shard_map/while/body/eval_jaxpr/axgs,kaygs->gkxys/dot_general | solution.py:100
  268.8 8.0 %convert_bitcast_fusion.2 = bf16[4,3,11,67,128]{3,2,1,4,0:T(8,128)(2,1)} fusion(bf16[3,4,4,4,128]{2,1,0,4,3:T(4,128)(2,1)} %copy.128, s32[4,4,128]{0,2,1:T(8,128)S(1)} %get-tuple-element.395, s32[4,4,128]{0,2,1:T(8,128)S(1)} %iota_add_fusion.6), kind=kOutput, calls=%fused_computation.1.clone.1 | convolution fusion | flops 14052864 | bytes 2329600 | tf_op jit(solution)/shard_map/while/body/eval_jaxpr/axgs,kaygs->gkxys/dot_general | solution.py:100
  301.1 8.0 %convert_bitcast_fusion.2 = bf16[4,3,11,67,128]{3,2,1,4,0:T(8,128)(2,1)} fusion(bf16[3,4,4,4,128]{2,1,0,4,3:T(4,128)(2,1)} %copy.128, s32[4,4,128]{0,2,1:T(8,128)S(1)} %get-tuple-element.395, s32[4,4,128]{0,2,1:T(8,128)S(1)} %iota_add_fusion.6), kind=kOutput, calls=%fused_computation.1.clone.1 | convolution fusion | flops 14052864 | bytes 2329600 | tf_op jit(solution)/shard_map/while/body/eval_jaxpr/axgs,kaygs->gkxys/dot_general | solution.py:100
  333.5 8.0 %convert_bitcast_fusion.2 = bf16[4,3,11,67,128]{3,2,1,4,0:T(8,128)(2,1)} fusion(bf16[3,4,4,4,128]{2,1,0,4,3:T(4,128)(2,1)} %copy.128, s32[4,4,128]{0,2,1:T(8,128)S(1)} %get-tuple-element.395, s32[4,4,128]{0,2,1:T(8,128)S(1)} %iota_add_fusion.6), kind=kOutput, calls=%fused_computation.1.clone.1 | convolution fusion | flops 14052864 | bytes 2329600 | tf_op jit(solution)/shard_map/while/body/eval_jaxpr/axgs,kaygs->gkxys/dot_general | solution.py:100
  365.8 8.0 %convert_bitcast_fusion.2 = bf16[4,3,11,67,128]{3,2,1,4,0:T(8,128)(2,1)} fusion(bf16[3,4,4,4,128]{2,1,0,4,3:T(4,128)(2,1)} %copy.128, s32[4,4,128]{0,2,1:T(8,128)S(1)} %get-tuple-element.395, s32[4,4,128]{0,2,1:T(8,128)S(1)} %iota_add_fusion.6), kind=kOutput, calls=%fused_computation.1.clone.1 | convolution fusion | flops 14052864 | bytes 2329600 | tf_op jit(solution)/shard_map/while/body/eval_jaxpr/axgs,kaygs->gkxys/dot_general | solution.py:100
  398.1 8.0 %convert_bitcast_fusion.2 = bf16[4,3,11,67,128]{3,2,1,4,0:T(8,128)(2,1)} fusion(bf16[3,4,4,4,128]{2,1,0,4,3:T(4,128)(2,1)} %copy.128, s32[4,4,128]{0,2,1:T(8,128)S(1)} %get-tuple-element.395, s32[4,4,128]{0,2,1:T(8,128)S(1)} %iota_add_fusion.6), kind=kOutput, calls=%fused_computation.1.clone.1 | convolution fusion | flops 14052864 | bytes 2329600 | tf_op jit(solution)/shard_map/while/body/eval_jaxpr/axgs,kaygs->gkxys/dot_general | solution.py:100
  430.5 8.0 %convert_bitcast_fusion.2 = bf16[4,3,11,67,128]{3,2,1,4,0:T(8,128)(2,1)} fusion(bf16[3,4,4,4,128]{2,1,0,4,3:T(4,128)(2,1)} %copy.128, s32[4,4,128]{0,2,1:T(8,128)S(1)} %get-tuple-element.395, s32[4,4,128]{0,2,1:T(8,128)S(1)} %iota_add_fusion.6), kind=kOutput, calls=%fused_computation.1.clone.1 | convolution fusion | flops 14052864 | bytes 2329600 | tf_op jit(solution)/shard_map/while/body/eval_jaxpr/axgs,kaygs->gkxys/dot_general | solution.py:100
  462.8 8.0 %convert_bitcast_fusion.2 = bf16[4,3,11,67,128]{3,2,1,4,0:T(8,128)(2,1)} fusion(bf16[3,4,4,4,128]{2,1,0,4,3:T(4,128)(2,1)} %copy.128, s32[4,4,128]{0,2,1:T(8,128)S(1)} %get-tuple-element.395, s32[4,4,128]{0,2,1:T(8,128)S(1)} %iota_add_fusion.6), kind=kOutput, calls=%fused_computation.1.clone.1 | convolution fusion | flops 14052864 | bytes 2329600 | tf_op jit(solution)/shard_map/while/body/eval_jaxpr/axgs,kaygs->gkxys/dot_general | solution.py:100
  495.1 8.0 %convert_bitcast_fusion.2 = bf16[4,3,11,67,128]{3,2,1,4,0:T(8,128)(2,1)} fusion(bf16[3,4,4,4,128]{2,1,0,4,3:T(4,128)(2,1)} %copy.128, s32[4,4,128]{0,2,1:T(8,128)S(1)} %get-tuple-element.395, s32[4,4,128]{0,2,1:T(8,128)S(1)} %iota_add_fusion.6), kind=kOutput, calls=%fused_computation.1.clone.1 | convolution fusion | flops 14052864 | bytes 2329600 | tf_op jit(solution)/shard_map/while/body/eval_jaxpr/axgs,kaygs->gkxys/dot_general | solution.py:100
  546.4 10.8 %all-to-all-start = ((f32[32,64,256]{2,0,1:T(8,128)}), f32[32,64,256]{2,0,1:T(8,128)}, u32[]{:S(2)}, u32[]{:S(2)}) async-start(f32[32,64,256]{2,0,1:T(8,128)} %fusion.63), calls=%async_computation | async-start | bytes 4194304 | tf_op jit(solution)/shard_map/all_to_all | solution.py:129
  559.4 26.5 %all-to-all-done = f32[32,64,256]{2,0,1:T(8,128)} async-done(((f32[32,64,256]{2,0,1:T(8,128)}), f32[32,64,256]{2,0,1:T(8,128)}, u32[]{:S(2)}, u32[]{:S(2)}) %all-to-all-start) | async-done | bytes 2097184 | tf_op jit(solution)/shard_map/all_to_all | solution.py:129
  592.6 33.5 %all_to_all.54 = f32[2,256,4,256]{3,2,0,1:T(4,128)S(1)} all-to-all(f32[2,256,4,256]{3,2,0,1:T(4,128)S(1)} %copy.79), channel_id=1, replica_groups=mesh['gx'=16,'gy'=8] {'gx'}, dimensions={1} | all-to-all | bytes 4194304 | tf_op jit(solution)/shard_map/all_to_all | solution.py:133
  628.3 28.2 %all_to_all.55 = f32[2,16,64,256]{3,2,0,1:T(8,128)S(1)} all-to-all(f32[2,16,64,256]{3,2,0,1:T(8,128)S(1)} %copy.82), channel_id=1, replica_groups=mesh['gx'=16,'gy'=8] {'gy'}, dimensions={1} | all-to-all | bytes 4194304 | tf_op jit(solution)/shard_map/all_to_all | solution.py:132
  656.7 10.9 %convolution_bitcast_fusion = f32[2,2,512,256]{2,3,1,0:T(8,128)S(1)} fusion(f32[2,2,512,256]{3,2,1,0:T(8,128)S(1)} %bitcast.185), kind=kOutput, calls=%fused_computation.47 | convolution fusion | flops 3224895488 | bytes 4194304 | tf_op jit(solution)/shard_map/qr,ckrz->ckqz/dot_general | solution.py:145
  667.6 11.2 %convolution_bitcast_fusion.1 = f32[2,2,512,256]{2,3,1,0:T(8,128)S(1)} fusion(f32[2,2,512,256]{3,2,1,0:T(8,128)S(1)} %bitcast.186), kind=kOutput, calls=%fused_computation.48 | convolution fusion | flops 3224895488 | bytes 4194304 | tf_op jit(solution)/shard_map/qr,ckrz->ckqz/dot_general | solution.py:142
  (276 shorter events, 392.5 us)
Async XLA Ops:
  0.0 684.1 %copy-start = (f32[8,256,256]{2,1,0:T(8,128)S(1)}, f32[8,256,256]{2,1,0:T(8,128)}, u32[]{:S(2)}) copy-start(f32[8,256,256]{2,1,0:T(8,128)} %param.17) | copy-start | bytes 6291460
  0.0 3.4 copy-start.2
  3.9 2.7 copy-start.1
  526.6 6.1 collective-permute-start
  538.7 6.2 collective-permute-start.1
  546.4 39.5 %all-to-all-start = ((f32[32,64,256]{2,0,1:T(8,128)}), f32[32,64,256]{2,0,1:T(8,128)}, u32[]{:S(2)}, u32[]{:S(2)}) async-start(f32[32,64,256]{2,0,1:T(8,128)} %fusion.63), calls=%async_computation | async-start | bytes 4194304 | tf_op jit(solution)/shard_map/all_to_all | solution.py:129
where the time goes:
time: 694 us; the launch traced here: 689 us
  matrix products  280 us (40%)
  other arithmetic  166 us (24%)
  local copies, waits for them, and re-layouts  95.3 us (14%)
  blocking collectives  61.8 us (9%)
  loops' own time  41.8 us (6%)
  waiting for transfers between devices  30 us (4%)
  starting transfers between devices  14.7 us (2%)
    dynamic_update_slice x64, other arithmetic, spread_turn(): lax.dynamic_update_slice(extended, current + pieces[member], (plane_start...  153 us
    dot_general x16, matrix products, spread_turn(): jnp.einsum('axgs,kaygs->gkxys', x_select, rows_y, preferred_element_type=...  128 us
    dot_general x16, matrix products, spread_turn(): jnp.einsum('gkxys,gksz->gxyz', window, z_window, preferred_element_type=j...  96.1 us
    dynamic_slice x32, local copies, waits for them, and re-layouts, spread_turn(): plane_part = lax.dynamic_slice_in_dim(planes, first_block, per_turn, 3)  50.7 us
    another operation x1, loops' own time, per_device(): lax.fori_loop(0, block_count // per_turn, spread_turn, jnp.zeros((cells_x...  41.8 us
    all_to_all x1, blocking collectives, per_device(): lax.all_to_all(spectrum, 'gx', split_axis=1, concat_axis=2, tiled=True)  33.5 us
    all_to_all x1, blocking collectives, per_device(): lax.all_to_all(lax.all_to_all(spectrum, 'gx', split_axis=1, concat_axis=2...  28.2 us
    all_to_all x1, waiting for transfers between devices, per_device(): lax.all_to_all(density, 'gx', split_axis=1, concat_axis=0, tiled=True)  26.5 us
  transfers between devices with their start and end apart: 3, of which 3 were waited for; matrix products, arithmetic and copies ran while one was open for 1% of the time, Pallas kernels for 0%

commit v1 on v0

v1 whole, which is shorter than its diff:
```python
import math

import jax
import jax.numpy as jnp
import ml_dtypes
import numpy as np
from jax import lax
from jax.experimental import pallas as pl
from jax.experimental.pallas import tpu as pltpu
from jax.sharding import PartitionSpec as P

NX = 512
NY = 512
NZ = 256
XB = 8
LANES = 128
MBLK = 8
KX = 256
TILE = 16
ROWS_Y = 80
WIN_X = XB + 3
F32 = jnp.float32
BF16 = jnp.bfloat16


def tap_constants(tap):
    def pick(c0, c1, c2, c3):
        return jnp.where(tap == 0, c0, jnp.where(tap == 1, c1, jnp.where(tap == 2, c2, c3))).astype(F32)

    return dict(
        shift=pick(1.0, 0.0, 0.0, 0.0),
        sign=pick(-1.0, 1.0, 1.0, 1.0),
        w=(pick(0.0, 2.0 / 3.0, 1.0 / 6.0, 0.0), pick(0.0, 0.0, 0.5, 0.0), pick(0.0, -1.0, 0.5, 0.0), pick(1.0 / 6.0, 0.5, -0.5, 1.0 / 6.0)),
        d=(pick(0.0, 0.0, 0.5, 0.0), pick(0.0, -2.0, 1.0, 0.0), pick(-0.5, 1.5, -1.5, 0.5)),
        s=(pick(0.0, -2.0, 1.0, 0.0), pick(1.0, 3.0, -3.0, 1.0)),
    )


def tap_values(fraction, const):
    u = const["shift"] + const["sign"] * fraction
    w0, w1, w2, w3 = const["w"]
    d0, d1, d2 = const["d"]
    s0, s1 = const["s"]
    return ((w3 * u + w2) * u + w1) * u + w0, (d2 * u + d1) * u + d0, s1 * u + s0


def spread_kernel(cells_x, cells_y, block_count, plane_ref, count_ref, moment_ref, fraction_ref, base_ref, out_ref, rim_ref,
                  raw, taps, a0, b0, a1, b1, density, stage, cursor, pair_group, pair_plane):
    planes = cells_x // XB
    spare = block_count + 2 * planes
    lane = lax.broadcasted_iota(jnp.int32, (TILE, LANES), 1)

    density[...] = jnp.zeros_like(density)

    for p in range(planes):
        cursor[p] = 0

    def tally(g, carry):
        p = plane_ref[g]
        cursor[p] = cursor[p] + count_ref[g]
        return carry

    lax.fori_loop(0, block_count, tally, 0)
    zero_group = jnp.zeros((TILE, LANES), F32)
    start = jnp.int32(0)
    pairs = jnp.int32(0)
    for p in range(planes):
        total = cursor[p]
        whole = (total + LANES - 1) // LANES
        cursor[p] = start * LANES
        raw[pl.ds(pl.multiple_of(start * TILE, TILE), TILE), :] = zero_group
        here = (whole + 1) // 2

        def note(i, carry, start=start, pairs=pairs, p=p):
            pair_group[pairs + i] = start + 2 * i
            pair_plane[pairs + i] = p
            return carry

        lax.fori_loop(0, here, note, 0)
        pairs = pairs + here
        start = start + total // LANES + 2
    for i in range(3):
        pair_group[pairs + i] = spare
        pair_plane[pairs + i] = 0
    for i in range(2):
        raw[(spare + i) * TILE:(spare + i + 1) * TILE, :] = zero_group

    def append(g, carry):
        p = plane_ref[g]
        live = count_ref[g]
        place = cursor[p]
        cursor[p] = place + live
        group = place // LANES
        offset = place % LANES
        column = pl.multiple_of(g * LANES, LANES)
        stage[0:10, :] = moment_ref[:, pl.ds(column, LANES)]
        stage[10:13, :] = fraction_ref[:, pl.ds(column, LANES)]
        stage[13:16, :] = base_ref[:, pl.ds(column, LANES)].astype(F32)
        rows = jnp.where(lane < live, stage[...], 0.0)
        rows = pltpu.roll(rows, offset, axis=1)
        first = pl.multiple_of(group * TILE, TILE)
        raw[pl.ds(first, TILE), :] = raw[pl.ds(first, TILE), :] + jnp.where(lane >= offset, rows, 0.0)
        raw[pl.ds(first + TILE, TILE), :] = jnp.where(lane < offset, rows, 0.0)
        return carry

    lax.fori_loop(0, block_count, append, 0)
    for p in range(planes):
        after = (cursor[p] + LANES - 1) // LANES
        raw[pl.ds(pl.multiple_of(after * TILE, TILE), TILE), :] = zero_group

    sub = lax.broadcasted_iota(jnp.int32, (8, LANES), 0)
    inner = tap_constants(sub % 4)
    outer = [tap_constants(sub // 4), tap_constants(2 + sub // 4)]
    tile_rows = lax.broadcasted_iota(jnp.int32, (TILE, LANES), 0).astype(F32).astype(BF16)
    none = jnp.zeros((TILE, LANES), BF16)

    def build(q, a_ref, b_ref, slot):
        for member in range(2):
            base = (pair_group[q] + member) * TILE
            first = (slot * 2 + member) * 64

            def row(r, base=base):
                return raw[pl.ds(base + r, 8, stride=0), :]

            def wide(r, base=base):
                return raw[pl.ds(base + r, TILE, stride=0), :].astype(BF16)

            def tap(r, first=first):
                return taps[pl.ds(first + r, TILE, stride=0), :].astype(BF16)

            m = [row(r) for r in range(10)]
            wx, dx, sx = tap_values(row(10), inner)
            x0 = m[0] * wx + m[1] * dx + m[4] * sx
            x1 = m[2] * wx + m[7] * dx
            x2 = m[5] * wx
            x3 = m[3] * wx + m[8] * dx
            x4 = m[9] * wx
            x5 = m[6] * wx
            for half in range(2):
                wy, dy, sy = tap_values(row(11), outer[half])
                taps[first + 8 * half:first + 8 * half + 8, :] = x0 * wy + x1 * dy + x2 * sy
                taps[first + 16 + 8 * half:first + 24 + 8 * half, :] = x3 * wy + x4 * dy
                taps[first + 32 + 8 * half:first + 40 + 8 * half, :] = x5 * wy
            wz, dz, sz = tap_values(row(12), inner)
            taps[first + 48:first + 52, :] = wz[0:4]
            taps[first + 52:first + 56, :] = dz[0:4]
            taps[first + 56:first + 60, :] = sz[0:4]

            zbase = wide(15)
            ztap = [[tap(48 + 4 * k + c) for c in range(4)] for k in range(3)]
            for t in range(NZ // TILE):
                gap = tile_rows + (TILE * t) - zbase
                hit = [gap == c for c in range(4)]
                for k in range(3):
                    value = none
                    for c in range(3, -1, -1):
                        value = jnp.where(hit[c], ztap[k][c], value)
                    b_ref[TILE * t:TILE * (t + 1), (member * 3 + k) * LANES:(member * 3 + k + 1) * LANES] = value

            ybase = wide(14)
            xbase = wide(13)
            bit2 = xbase >= 4
            xbase = xbase - jnp.where(bit2, jnp.full_like(none, 4), none)
            bit1 = xbase >= 2
            xbase = xbase - jnp.where(bit1, jnp.full_like(none, 2), none)
            bit0 = xbase >= 1
            for t in range(ROWS_Y // TILE):
                gap = tile_rows + (TILE * t) - ybase
                hit = [gap == c for c in range(4)]
                for k in range(3):
                    column = []
                    for a in range(4):
                        value = none
                        for b in range(3, -1, -1):
                            value = jnp.where(hit[b], tap(16 * k + 4 * b + a), value)
                        column.append(value)
                    for bit, step in ((bit0, 1), (bit1, 2), (bit2, 4)):
                        size = len(column)
                        column = [
                            jnp.where(bit, column[i - step] if i >= step else none, column[i] if i < size else none)
                            for i in range(size + step)
                        ]
                    for x in range(WIN_X):
                        a_ref[x * ROWS_Y + TILE * t:x * ROWS_Y + TILE * (t + 1),
                              (member * 3 + k) * LANES:(member * 3 + k + 1) * LANES] = column[x]

    def spread(q, a_ref, b_ref):
        first = pl.multiple_of(pair_plane[q] * (XB * ROWS_Y), XB * ROWS_Y)
        part = lax.dot_general(a_ref[...], b_ref[...], (((1,), (1,)), ((), ())), preferred_element_type=F32)
        for half in range(2):
            grid = density.at[half]
            grid[pl.ds(first, WIN_X * ROWS_Y), :] = (
                grid[pl.ds(first, WIN_X * ROWS_Y), :] + part[:, half * LANES:(half + 1) * LANES]
            )

    build(0, a0, b0, 0)

    def turn(i, carry):
        build(2 * i + 1, a1, b1, 1)
        spread(2 * i, a0, b0)
        build(2 * i + 2, a0, b0, 0)
        spread(2 * i + 1, a1, b1)
        return carry

    lax.fori_loop(0, (pairs + 1) // 2, turn, 0)

    lines = cells_x + 3
    width = out_ref.shape[1] // lines
    columns = width // 2
    for y in range(cells_y + 3):
        for half in range(2):
            value = density.at[half][pl.ds(y, lines, stride=ROWS_Y), :]
            if y < cells_y:
                out_ref[y // columns, pl.ds(y % columns * 2 + half, lines, stride=width), :] = value
            else:
                rim_ref[pl.ds((y - cells_y) * 2 + half, lines, stride=width), :] = value
    for r in range(6, width):
        rim_ref[pl.ds(r, lines, stride=width), :] = jnp.zeros((lines, LANES), F32)


def x_kernel(groups, cells_x, in_ref, high_ref, low_ref, out_ref, lines, narrow):
    width = 8
    for l in range(width):
        cut = slice(l * LANES, (l + 1) * LANES)
        for src in range(groups):
            lines[src * cells_x:(src + 1) * cells_x, cut] = in_ref[src, pl.ds(l, cells_x, stride=width), :]
        for src in range(groups):
            first = (src + 1) % groups * cells_x
            lines[first:first + 3, cut] = lines[first:first + 3, cut] + in_ref[src, pl.ds(cells_x * width + l, 3, stride=width), :]
    narrow[...] = lines[...].astype(BF16)
    data = narrow[...]
    result = jnp.dot(high_ref[...], data, preferred_element_type=F32) + jnp.dot(low_ref[...], data, preferred_element_type=F32)
    devices = out_ref.shape[0] // 32
    for q in range(4):
        for l in range(width):
            out_ref[pl.ds(l // 2 * 8 + q * 2 + l % 2, devices, stride=32), :] = (
                result[q * devices:(q + 1) * devices, l * LANES:(l + 1) * LANES]
            )


def y_kernel(in_ref, high_ref, low_ref, coupling_ref, out_ref, data, spectrum):
    @pl.when(pl.program_id(0) == 0)
    def _():
        for q in range(4):
            for half in range(2):
                value = in_ref[pl.ds(q * 2 + half, NY, stride=8), :]
                same = slice(q * NZ + half * LANES, q * NZ + (half + 1) * LANES)
                swap = slice((q ^ 1) * NZ + half * LANES, (q ^ 1) * NZ + (half + 1) * LANES)
                data[0:NY, same] = value.astype(BF16)
                data[NY:2 * NY, swap] = (value if q % 2 else -value).astype(BF16)
        lines = data[...]
        spectrum[...] = jnp.dot(high_ref[...], lines, preferred_element_type=F32) + jnp.dot(
            low_ref[...], lines, preferred_element_type=F32
        )

    block = NY // MBLK
    rows = spectrum[pl.ds(pl.multiple_of(pl.program_id(0) * block, block), block), :].astype(BF16)
    rows = jnp.concatenate([rows[:, q * NZ:(q + 1) * NZ] for q in range(4)], axis=0)
    weight = coupling_ref[0]
    high = weight.astype(BF16)
    low = (weight - high.astype(F32)).astype(BF16)
    dims = (((1,), (1,)), ((), ()))
    result = lax.dot_general(rows, high, dims, preferred_element_type=F32) + lax.dot_general(
        rows, low, dims, preferred_element_type=F32
    )
    for q in range(4):
        out_ref[q % 2, q // 2, :, :] = result[q * block:(q + 1) * block]


def two_parts(table):
    high = table.astype(ml_dtypes.bfloat16)
    low = (table - high.astype(np.float64)).astype(ml_dtypes.bfloat16)
    return high, low


def tables(size_x, size_y):
    devices = size_x * size_y
    wave = np.arange(KX).reshape(devices, 2).T.reshape(2, 1, devices, 1)
    angle = 2.0 * np.pi * (wave * np.arange(NX) % NX) / NX
    scale = 1.0 / math.sqrt(NX * NY)
    table_x = np.concatenate([np.cos(angle), -np.sin(angle)], 1).reshape(4 * devices, NX) * scale
    columns = NY // devices
    y = np.arange(size_y)[None, :, None] * (NY // size_y) + np.arange(size_x)[:, None, None] * columns + np.arange(columns)
    angle = 2.0 * np.pi * (np.arange(NY)[:, None] * y.reshape(1, NY) % NY) / NY
    table_y = np.concatenate([np.cos(angle), np.sin(angle)], 1)
    return two_parts(table_x), two_parts(table_y)


def per_device(multipoles, fractions, base_index, block_plane, atom_count, coupling):
    size_x = lax.axis_size("gx")
    size_y = lax.axis_size("gy")
    cells_x = NX // size_x
    cells_y = NY // size_y
    block_count = block_plane.shape[0]
    devices = size_x * size_y
    lines = cells_x + 3
    (x_high, x_low), (y_high, y_low) = tables(size_x, size_y)
    groups = block_count + 2 * (cells_x // XB) + 2
    vmem = pltpu.VMEM
    smem = pl.BlockSpec(memory_space=pltpu.SMEM)
    whole = pl.BlockSpec(memory_space=pltpu.VMEM)
    limit = pltpu.CompilerParams(vmem_limit_bytes=56 << 20)

    density, rim = pl.pallas_call(
        lambda *refs: spread_kernel(cells_x, cells_y, block_count, *refs),
        out_shape=(
            jax.ShapeDtypeStruct((size_x, lines * 8, LANES), F32),
            jax.ShapeDtypeStruct((lines * 8, LANES), F32),
        ),
        in_specs=[smem, smem, whole, whole, whole],
        out_specs=(whole, whole),
        scratch_shapes=[
            vmem((groups * TILE, LANES), F32),
            vmem((256, LANES), F32),
            vmem((WIN_X * ROWS_Y, 6 * LANES), BF16),
            vmem((NZ, 6 * LANES), BF16),
            vmem((WIN_X * ROWS_Y, 6 * LANES), BF16),
            vmem((NZ, 6 * LANES), BF16),
            vmem((2, lines * ROWS_Y, LANES), F32),
            vmem((TILE, LANES), F32),
            pltpu.SMEM((8,), jnp.int32),
            pltpu.SMEM((block_count + 16,), jnp.int32),
            pltpu.SMEM((block_count + 16,), jnp.int32),
        ],
        compiler_params=limit,
        name="spread",
    )(block_plane, atom_count, multipoles, fractions, base_index)

    rim = lax.ppermute(rim, "gy", [(i, (i + 1) % size_y) for i in range(size_y)])
    density = density.at[0].add(rim)
    density = lax.all_to_all(density, "gx", split_axis=0, concat_axis=0, tiled=True)

    spectrum = pl.pallas_call(
        lambda *refs: x_kernel(size_x, cells_x, *refs),
        out_shape=jax.ShapeDtypeStruct((devices * 32, LANES), F32),
        in_specs=[whole] * 3,
        out_specs=whole,
        scratch_shapes=[vmem((NX, 8 * LANES), F32), vmem((NX, 8 * LANES), BF16)],
        compiler_params=limit,
        name="transform_x",
    )(density, jnp.asarray(x_high), jnp.asarray(x_low))

    spectrum = lax.all_to_all(
        spectrum.reshape(devices, 32, LANES), ("gx", "gy"), split_axis=0, concat_axis=0, tiled=True
    ).reshape(devices * 32, LANES)

    fixed = lambda i: (0, 0)
    return pl.pallas_call(
        y_kernel,
        out_shape=jax.ShapeDtypeStruct((2, 2, NY, NZ), F32),
        grid=(MBLK,),
        in_specs=[
            pl.BlockSpec((devices * 32, LANES), fixed, pipeline_mode=pl.Buffered(1)),
            pl.BlockSpec((NY, 2 * NY), fixed, pipeline_mode=pl.Buffered(1)),
            pl.BlockSpec((NY, 2 * NY), fixed, pipeline_mode=pl.Buffered(1)),
            pl.BlockSpec((1, NZ, NZ), lambda i: (i, 0, 0)),
        ],
        out_specs=pl.BlockSpec((2, 2, NY // MBLK, NZ), lambda i: (0, 0, i, 0)),
        scratch_shapes=[vmem((2 * NY, 4 * NZ), BF16), vmem((NY, 4 * NZ), F32)],
        compiler_params=limit,
        name="transform_y",
    )(spectrum, jnp.asarray(y_high), jnp.asarray(y_low), coupling)


def solution(mesh):
    return jax.shard_map(
        per_device,
        mesh=mesh,
        in_specs=(
            P(None, ("gx", "gy")),
            P(None, ("gx", "gy")),
            P(None, ("gx", "gy")),
            P(("gx", "gy")),
            P(("gx", "gy")),
            P(),
        ),
        out_specs=P(None, ("gx", "gy"), None, None),
        check_vma=False,
    )
```

time: 694 us -> 129 us (0.19)
  matrix products: 280 us -> 0 us
  other arithmetic: 166 us -> 1.58 us
  local copies, waits for them, and re-layouts: 95.3 us -> 0 us
  Pallas kernels: 0 us -> 44.7 us
  loops' own time: 41.8 us -> 0 us
  waiting for transfers between devices: 30 us -> 4.12 us
  blocking collectives: 61.8 us -> 75.8 us
  starting transfers between devices: 14.7 us -> 2.15 us
    dot_general x52 -> x0, matrix products: 280 us -> none  [the longest x16 128 us: spread_turn(): jnp.einsum('axgs,kaygs->gkxys', x_select, rows_y, preferred_element_type=...]
    dynamic_update_slice x64 -> x0, other arithmetic: 153 us -> none  [spread_turn(): lax.dynamic_update_slice(extended, current + pieces[member], (plane_start...]
    dynamic_slice x80 -> x0, local copies, waits for them, and re-layouts: 66.9 us -> none  [the longest x32 50.7 us: spread_turn(): plane_part = lax.dynamic_slice_in_dim(planes, first_block, per_turn, 3)]
    pallas_call x0 -> x3, Pallas kernels: none -> 44.7 us  [the longest x1 28.4 us: per_device(): pl.pallas_call(lambda *refs: spread_kernel(cells_x, cells_y, block_count,...]
    another operation x1 -> x0, loops' own time: 41.8 us -> none  [per_device(): lax.fori_loop(0, block_count // per_turn, spread_turn, jnp.zeros((cells_x...]
    all_to_all x1 -> x0, waiting for transfers between devices: 26.5 us -> none  [per_device(): lax.all_to_all(density, 'gx', split_axis=1, concat_axis=0, tiled=True)]
    all_to_all x2, blocking collectives: 61.8 us -> 75.8 us  [the longest x1 40.8 us: per_device(): lax.all_to_all(density, 'gx', split_axis=0, concat_axis=0, tiled=True)]
    all_to_all x1 -> x0, starting transfers between devices: 10.8 us -> none  [per_device(): lax.all_to_all(density, 'gx', split_axis=1, concat_axis=0, tiled=True)]
  transfers between devices with their start and end apart: 3 -> 1, of which waited for: 3 -> 1; matrix products, arithmetic and copies ran while one was open for 1% -> 0% of each run, Pallas kernels for 0% -> 0%
where the time goes in v1:
time: 129 us; the launch traced here: 128 us
  blocking collectives  75.8 us (59%)
  Pallas kernels  44.7 us (35%)
  waiting for transfers between devices  4.12 us (3%)
  starting transfers between devices  2.15 us (2%)
  other arithmetic  1.58 us (1%)
    all_to_all x1, blocking collectives, per_device(): lax.all_to_all(density, 'gx', split_axis=0, concat_axis=0, tiled=True)  40.8 us
    all_to_all x1, blocking collectives, per_device(): lax.all_to_all(spectrum.reshape(devices, 32, LANES), ('gx', 'gy'), split_...  35 us
    pallas_call x1, Pallas kernels, per_device(): pl.pallas_call(lambda *refs: spread_kernel(cells_x, cells_y, block_count,...  28.4 us
    pallas_call x1, Pallas kernels, per_device(): pl.pallas_call(y_kernel, out_shape=jax.ShapeDtypeStruct((2, 2, NY, NZ), F...  10.5 us
    pallas_call x1, Pallas kernels, per_device(): pl.pallas_call(lambda *refs: x_kernel(size_x, cells_x, *refs), out_shape=...  5.72 us
    ppermute x1, waiting for transfers between devices, per_device(): lax.ppermute(rim, 'gy', [(i, (i + 1) % size_y) for i in range(size_y)])  4.12 us
  transfers between devices with their start and end apart: 1, of which 1 were waited for; matrix products, arithmetic and copies ran while one was open for 0% of the time, Pallas kernels for 0%

profile of v1, /device:TPU:1, one launch (start us, length us, event | category | flops | bytes accessed | tf_op | source)
XLA Modules:
  0.0 128.4 jit_solution(18063712712950708084)
XLA Ops:
  0.0 28.4 %spread.1 = (f32[16,280,128]{2,1,0:T(8,128)}, f32[280,128]{1,0:T(8,128)}) custom-call(s32[64]{0:T(128)} %refs_0_.1, s32[64]{0:T(128)} %refs_1_.2, f32[10,8192]{1,0:T(8,128)} %refs_2_.2, f32[3,8192]{1,0:T(4,128)} %refs_3_.1, s32[3,8192]{1,0:T(4,128)} %refs_4_.1), custom_call_target="tpu_custom_call" | custom-call | tf_op jit(solution)/shard_map/spread/pallas_call | solution.py:304
  28.4 2.1 %collective-permute-start = (f32[280,128]{1,0:T(8,128)}, f32[280,128]{1,0:T(8,128)S(1)}, u32[]{:S(2)}, u32[]{:S(2)}) collective-permute-start(f32[280,128]{1,0:T(8,128)} %get-tuple-element.20), channel_id=1, source_target_pairs={{0,1},{1,2},{2,3},{3,4},{4,5},{5,6},{6,7},{7,0},{8,9},{9,10},{10,1... | collective-permute-start | bytes 430088 | tf_op jit(solution)/shard_map/ppermute | solution.py:329
  30.6 4.1 %collective-permute-done = f32[280,128]{1,0:T(8,128)S(1)} collective-permute-done((f32[280,128]{1,0:T(8,128)}, f32[280,128]{1,0:T(8,128)S(1)}, u32[]{:S(2)}, u32[]{:S(2)}) %collective-permute-start) | collective-permute-done | bytes 143392 | tf_op jit(solution)/shard_map/ppermute | solution.py:329
  34.7 1.6 %fusion = f32[16,280,128]{2,1,0:T(8,128)} fusion(f32[16,280,128]{2,1,0:T(8,128)} %get-tuple-element.19, f32[280,128]{1,0:T(8,128)S(1)} %collective-permute-done), kind=kLoop, calls=%fused_computation.1 | loop fusion | flops 35840 | bytes 430080 | tf_op jit(solution)/shard_map/scatter-add | solution.py:330
  36.3 40.8 %all_to_all.10.refs_0_ = f32[16,280,128]{2,1,0:T(8,128)} all-to-all(f32[16,280,128]{2,1,0:T(8,128)} %fusion), channel_id=1, replica_groups=mesh['gx'=16,'gy'=8] {'gx'}, dimensions={0} | all-to-all | bytes 4587520 | tf_op jit(solution)/shard_map/all_to_all | solution.py:331
  77.1 5.7 %transform_x.1 = f32[4096,128]{1,0:T(8,128)} custom-call(f32[16,280,128]{2,1,0:T(8,128)} %all_to_all.10.refs_0_, bf16[512,512]{1,0:T(8,128)(2,1)} %constant.35.clone.refs_1_, bf16[512,512]{1,0:T(8,128)(2,1)} %constant.36.clone.refs_2_), custom_call_target="tpu_custom_call" | custom-call | tf_op jit(solution)/shard_map/transform_x/pallas_call | solution.py:333
  82.8 35.0 %all_to_all.11 = f32[128,32,128]{2,1,0:T(8,128)} all-to-all(f32[128,32,128]{2,1,0:T(8,128)} %bitcast.6), channel_id=1, replica_groups=mesh['gx'=16,'gy'=8] {'gx','gy'}, dimensions={0} | all-to-all | bytes 4194304 | tf_op jit(solution)/shard_map/all_to_all | solution.py:343
  117.8 10.5 %transform_y.1 = f32[2,2,512,256]{3,2,1,0:T(8,128)} custom-call(f32[4096,128]{1,0:T(8,128)} %bitcast.7, bf16[512,1024]{1,0:T(8,128)(2,1)} %constant.37.clone.high_ref, bf16[512,1024]{1,0:T(8,128)(2,1)} %constant.38.clone.low_ref, f32[8,256,256]{2,1,0:T(8,128)} %coupling_ref.1), custom_call_target="tpu_custom_call" | custom-call | tf_op jit(solution)/shard_map/transform_y/pallas_call | solution.py:348
Async XLA Ops:
  28.4 6.3 %collective-permute-start = (f32[280,128]{1,0:T(8,128)}, f32[280,128]{1,0:T(8,128)S(1)}, u32[]{:S(2)}, u32[]{:S(2)}) collective-permute-start(f32[280,128]{1,0:T(8,128)} %get-tuple-element.20), channel_id=1, source_target_pairs={{0,1},{1,2},{2,3},{3,4},{4,5},{5,6},{6,7},{7,0},{8,9},{9,10},{10,1... | collective-permute-start | bytes 430088 | tf_op jit(solution)/shard_map/ppermute | solution.py:329

commit v2 on v1

--- a/solution.py
+++ b/solution.py
@@ -17,8 +17,12 @@
 MBLK = 8
 KX = 256
 TILE = 16
-ROWS_Y = 80
+ROWS_Y = 64
 WIN_X = XB + 3
+ROWS = WIN_X * ROWS_Y + 3 * TILE
+BATCH = 8
+BUILD_STEPS = 3
+CHUNKS = ((0, 128), (128, 128), (256, 128), (384, 128), (512, 128), (640, 112))
 F32 = jnp.float32
 BF16 = jnp.bfloat16
 
@@ -44,13 +48,31 @@
     return ((w3 * u + w2) * u + w1) * u + w0, (d2 * u + d1) * u + d0, s1 * u + s0
 
 
-def spread_kernel(cells_x, cells_y, block_count, plane_ref, count_ref, moment_ref, fraction_ref, base_ref, out_ref, rim_ref,
-                  raw, taps, a0, b0, a1, b1, density, stage, cursor, pair_group, pair_plane):
+def spread_kernel(cells_x, cells_y, block_count, plane_in, count_in, moment_in, fraction_in, base_in, out_ref, rim_ref,
+                  plane_ref, count_ref, moment_ref, fraction_ref, base_ref, arrived, raw, taps, a0, b0, a1, b1, density, edge, stage, cursor, pair_group, pair_plane, pair_last):
     planes = cells_x // XB
     spare = block_count + 2 * planes
     lane = lax.broadcasted_iota(jnp.int32, (TILE, LANES), 1)
 
+    copies = [
+        pltpu.make_async_copy(source, target, arrived.at[i])
+        for i, (source, target) in enumerate(
+            (
+                (plane_in, plane_ref),
+                (count_in, count_ref),
+                (moment_in, moment_ref),
+                (fraction_in, fraction_ref),
+                (base_in, base_ref),
+            )
+        )
+    ]
+    for copy in copies:
+        copy.start()
     density[...] = jnp.zeros_like(density)
+    edge[...] = jnp.zeros_like(edge)
+
+    copies[0].wait()
+    copies[1].wait()
 
     for p in range(planes):
         cursor[p] = 0
@@ -71,9 +93,10 @@
         raw[pl.ds(pl.multiple_of(start * TILE, TILE), TILE), :] = zero_group
         here = (whole + 1) // 2
 
-        def note(i, carry, start=start, pairs=pairs, p=p):
+        def note(i, carry, start=start, pairs=pairs, here=here, p=p):
             pair_group[pairs + i] = start + 2 * i
             pair_plane[pairs + i] = p
+            pair_last[pairs + i] = jnp.where(i == here - 1, 1, 0)
             return carry
 
         lax.fori_loop(0, here, note, 0)
@@ -82,28 +105,36 @@
     for i in range(3):
         pair_group[pairs + i] = spare
         pair_plane[pairs + i] = 0
+        pair_last[pairs + i] = 1
     for i in range(2):
         raw[(spare + i) * TILE:(spare + i + 1) * TILE, :] = zero_group
 
-    def append(g, carry):
-        p = plane_ref[g]
-        live = count_ref[g]
-        place = cursor[p]
-        cursor[p] = place + live
-        group = place // LANES
-        offset = place % LANES
-        column = pl.multiple_of(g * LANES, LANES)
-        stage[0:10, :] = moment_ref[:, pl.ds(column, LANES)]
-        stage[10:13, :] = fraction_ref[:, pl.ds(column, LANES)]
-        stage[13:16, :] = base_ref[:, pl.ds(column, LANES)].astype(F32)
-        rows = jnp.where(lane < live, stage[...], 0.0)
-        rows = pltpu.roll(rows, offset, axis=1)
-        first = pl.multiple_of(group * TILE, TILE)
-        raw[pl.ds(first, TILE), :] = raw[pl.ds(first, TILE), :] + jnp.where(lane >= offset, rows, 0.0)
-        raw[pl.ds(first + TILE, TILE), :] = jnp.where(lane < offset, rows, 0.0)
+    for copy in copies[2:]:
+        copy.wait()
+
+    def append(i, carry):
+        moved = []
+        for k in range(BATCH):
+            g = i * BATCH + k
+            column = pl.multiple_of(g * LANES, LANES)
+            stage[k, 0:10, :] = moment_ref[:, pl.ds(column, LANES)]
+            stage[k, 10:13, :] = fraction_ref[:, pl.ds(column, LANES)]
+            stage[k, 13:16, :] = base_ref[:, pl.ds(column, LANES)].astype(F32)
+        for k in range(BATCH):
+            g = i * BATCH + k
+            p = plane_ref[g]
+            live = count_ref[g]
+            place = cursor[p]
+            cursor[p] = place + live
+            offset = place % LANES
+            rows = pltpu.roll(jnp.where(lane < live, stage[k], 0.0), offset, axis=1)
+            moved.append((pl.multiple_of(place // LANES * TILE, TILE), lane >= offset, rows))
+        for first, keep, rows in moved:
+            raw[pl.ds(first, TILE), :] = raw[pl.ds(first, TILE), :] + jnp.where(keep, rows, 0.0)
+            raw[pl.ds(first + TILE, TILE), :] = jnp.where(keep, 0.0, rows)
         return carry
 
-    lax.fori_loop(0, block_count, append, 0)
+    lax.fori_loop(0, block_count // BATCH, append, 0)
     for p in range(planes):
         after = (cursor[p] + LANES - 1) // LANES
         raw[pl.ds(pl.multiple_of(after * TILE, TILE), TILE), :] = zero_group
@@ -113,6 +144,9 @@
     outer = [tap_constants(sub // 4), tap_constants(2 + sub // 4)]
     tile_rows = lax.broadcasted_iota(jnp.int32, (TILE, LANES), 0).astype(F32).astype(BF16)
     none = jnp.zeros((TILE, LANES), BF16)
+    tile_iota = lax.broadcasted_iota(jnp.int32, (TILE, LANES), 0)
+    edge_x = (tile_iota // 4).astype(F32).astype(BF16)
+    edge_y = (cells_y + tile_iota % 4).astype(F32).astype(BF16)
 
     def build(q, a_ref, b_ref, slot):
         for member in range(2):
@@ -156,9 +190,27 @@
                     for c in range(3, -1, -1):
                         value = jnp.where(hit[c], ztap[k][c], value)
                     b_ref[TILE * t:TILE * (t + 1), (member * 3 + k) * LANES:(member * 3 + k + 1) * LANES] = value
+                yield
 
             ybase = wide(14)
             xbase = wide(13)
+            gap = edge_y - ybase
+            hit = [gap == c for c in range(4)]
+            where_x = [[edge_x + 4 * m - xbase == c for c in range(4)] for m in range(3)]
+            for k in range(3):
+                column = []
+                for a in range(4):
+                    value = none
+                    for b in range(3, -1, -1):
+                        value = jnp.where(hit[b], tap(16 * k + 4 * b + a), value)
+                    column.append(value)
+                for m in range(3):
+                    value = none
+                    for a in range(3, -1, -1):
+                        value = jnp.where(where_x[m][a], column[a], value)
+                    a_ref[WIN_X * ROWS_Y + TILE * m:WIN_X * ROWS_Y + TILE * (m + 1),
+                          (member * 3 + k) * LANES:(member * 3 + k + 1) * LANES] = value
+                yield
             bit2 = xbase >= 4
             xbase = xbase - jnp.where(bit2, jnp.full_like(none, 4), none)
             bit1 = xbase >= 2
@@ -183,37 +235,81 @@
                     for x in range(WIN_X):
                         a_ref[x * ROWS_Y + TILE * t:x * ROWS_Y + TILE * (t + 1),
                               (member * 3 + k) * LANES:(member * 3 + k + 1) * LANES] = column[x]
-
-    def spread(q, a_ref, b_ref):
-        first = pl.multiple_of(pair_plane[q] * (XB * ROWS_Y), XB * ROWS_Y)
-        part = lax.dot_general(a_ref[...], b_ref[...], (((1,), (1,)), ((), ())), preferred_element_type=F32)
-        for half in range(2):
-            grid = density.at[half]
-            grid[pl.ds(first, WIN_X * ROWS_Y), :] = (
-                grid[pl.ds(first, WIN_X * ROWS_Y), :] + part[:, half * LANES:(half + 1) * LANES]
-            )
-
-    build(0, a0, b0, 0)
-
-    def turn(i, carry):
-        build(2 * i + 1, a1, b1, 1)
-        spread(2 * i, a0, b0)
-        build(2 * i + 2, a0, b0, 0)
-        spread(2 * i + 1, a1, b1)
-        return carry
-
-    lax.fori_loop(0, (pairs + 1) // 2, turn, 0)
+                    yield
+
+    def multiply(sums, a_ref, b_ref):
+        def push(part, unit, register):
+            cut = slice(part * 2 * LANES, (part + 1) * 2 * LANES)
+            pltpu.matmul_push_rhs(b_ref[:, cut], register, unit, transpose=True)
+
+        def add(part, unit, i, register):
+            row, size = CHUNKS[i]
+            lhs = a_ref[row:row + size, part * 2 * LANES:(part + 1) * 2 * LANES]
+            pltpu.matmul_acc_lhs(sums[unit * len(CHUNKS) + i], lhs, load_staged_rhs=register)
+
+        push(0, 0, 0)
+        push(1, 1, 0)
+        yield
+        for i in range(len(CHUNKS)):
+            for unit in range(2):
+                add(unit, unit, i, None if i else 0)
+                yield
+            if i < 2:
+                push(2, i, 1)
+        for i in range(len(CHUNKS) // 2):
+            for unit in range(2):
+                add(2, unit, i + unit * (len(CHUNKS) // 2), None if i else 1)
+                yield
+
+    def flush(sums, plane):
+        main = WIN_X * ROWS_Y
+        first = pl.multiple_of(plane * (XB * ROWS_Y), XB * ROWS_Y)
+        corner = pl.multiple_of(plane * (XB * 4), XB * 4)
+        for i, (row, size) in enumerate(CHUNKS):
+            part = pltpu.matmul_pop(sums[i]) + pltpu.matmul_pop(sums[len(CHUNKS) + i])
+            inside = min(size, main - row)
+            for half in range(2):
+                cut = slice(half * LANES, (half + 1) * LANES)
+                grid, rim = density.at[half], edge.at[half]
+                grid[pl.ds(first + row, inside), :] = grid[pl.ds(first + row, inside), :] + part[:inside, cut]
+                if inside < size:
+                    rim[pl.ds(corner, size - inside), :] = rim[pl.ds(corner, size - inside), :] + part[inside:, cut]
+
+    def step(sums, q, now, later, slot):
+        steps = multiply(sums, *now)
+        for i, _ in enumerate(build(q + 1, *later, slot)):
+            if i % BUILD_STEPS == 0:
+                next(steps, None)
+        for _ in steps:
+            pass
+
+        @pl.when(pair_last[q] == 1)
+        def _():
+            flush(sums, pair_plane[q])
+
+    for _ in build(0, a0, b0, 0):
+        pass
+
+    def turns(*sums):
+        def turn(i, carry):
+            step(sums, 2 * i, (a0, b0), (a1, b1), 1)
+            step(sums, 2 * i + 1, (a1, b1), (a0, b0), 0)
+            return carry
+
+        lax.fori_loop(0, (pairs + 1) // 2, turn, 0)
+
+    pl.run_scoped(turns, *[pltpu.ACC(unit)((size, NZ), F32) for unit in range(2) for _, size in CHUNKS])
 
     lines = cells_x + 3
     width = out_ref.shape[1] // lines
     columns = width // 2
-    for y in range(cells_y + 3):
-        for half in range(2):
-            value = density.at[half][pl.ds(y, lines, stride=ROWS_Y), :]
-            if y < cells_y:
-                out_ref[y // columns, pl.ds(y % columns * 2 + half, lines, stride=width), :] = value
-            else:
-                rim_ref[pl.ds((y - cells_y) * 2 + half, lines, stride=width), :] = value
+    for half in range(2):
+        for y in range(cells_y):
+            out_ref[y // columns, pl.ds(y % columns * 2 + half, lines, stride=width), :] = (
+                density.at[half][pl.ds(y, lines, stride=ROWS_Y), :]
+            )
+        for y in range(3):
+            rim_ref[pl.ds(y * 2 + half, lines, stride=width), :] = edge.at[half][pl.ds(y, lines, stride=4), :]
     for r in range(6, width):
         rim_ref[pl.ds(r, lines, stride=width), :] = jnp.zeros((lines, LANES), F32)
 
@@ -241,20 +337,27 @@
 def y_kernel(in_ref, high_ref, low_ref, coupling_ref, out_ref, data, spectrum):
     @pl.when(pl.program_id(0) == 0)
     def _():
-        for q in range(4):
-            for half in range(2):
-                value = in_ref[pl.ds(q * 2 + half, NY, stride=8), :]
-                same = slice(q * NZ + half * LANES, q * NZ + (half + 1) * LANES)
-                swap = slice((q ^ 1) * NZ + half * LANES, (q ^ 1) * NZ + (half + 1) * LANES)
-                data[0:NY, same] = value.astype(BF16)
-                data[NY:2 * NY, swap] = (value if q % 2 else -value).astype(BF16)
-        lines = data[...]
-        spectrum[...] = jnp.dot(high_ref[...], lines, preferred_element_type=F32) + jnp.dot(
-            low_ref[...], lines, preferred_element_type=F32
-        )
+        half_y = NY // 2
+        sums = []
+        for odd in range(2):
+            for q in range(4):
+                for half in range(2):
+                    value = in_ref[pl.ds(odd * 8 + q * 2 + half, half_y, stride=16), :]
+                    same = slice(q * NZ + half * LANES, q * NZ + (half + 1) * LANES)
+                    swap = slice((q ^ 1) * NZ + half * LANES, (q ^ 1) * NZ + (half + 1) * LANES)
+                    data[odd, 0:half_y, same] = value.astype(BF16)
+                    data[odd, half_y:NY, swap] = (value if q % 2 else -value).astype(BF16)
+            lines = data[odd]
+            sums.append(
+                jnp.dot(high_ref[odd], lines, preferred_element_type=F32)
+                + jnp.dot(low_ref[odd], lines, preferred_element_type=F32)
+            )
+        even, odd = sums
+        spectrum[0:half_y, :] = (even + odd).astype(BF16)
+        spectrum[half_y:NY, :] = (even - odd).astype(BF16)
 
     block = NY // MBLK
-    rows = spectrum[pl.ds(pl.multiple_of(pl.program_id(0) * block, block), block), :].astype(BF16)
+    rows = spectrum[pl.ds(pl.multiple_of(pl.program_id(0) * block, block), block), :]
     rows = jnp.concatenate([rows[:, q * NZ:(q + 1) * NZ] for q in range(4)], axis=0)
     weight = coupling_ref[0]
     high = weight.astype(BF16)
@@ -281,9 +384,50 @@
     table_x = np.concatenate([np.cos(angle), -np.sin(angle)], 1).reshape(4 * devices, NX) * scale
     columns = NY // devices
     y = np.arange(size_y)[None, :, None] * (NY // size_y) + np.arange(size_x)[:, None, None] * columns + np.arange(columns)
-    angle = 2.0 * np.pi * (np.arange(NY)[:, None] * y.reshape(1, NY) % NY) / NY
-    table_y = np.concatenate([np.cos(angle), np.sin(angle)], 1)
+    y = y.reshape(NY // 2, 2).T.reshape(2, 1, NY // 2)
+    angle = 2.0 * np.pi * (np.arange(NY // 2)[None, :, None] * y % NY) / NY
+    table_y = np.concatenate([np.cos(angle), np.sin(angle)], 2)
     return two_parts(table_x), two_parts(table_y)
+
+
+def make_spread(block_count, cells_x, cells_y, size_x):
+    lines = cells_x + 3
+    groups = block_count + 2 * (cells_x // XB) + 2
+    vmem = pltpu.VMEM
+    slots = block_count * LANES
+    whole = pl.BlockSpec(memory_space=pltpu.VMEM)
+    return pl.pallas_call(
+        lambda *refs: spread_kernel(cells_x, cells_y, block_count, *refs),
+        out_shape=(
+            jax.ShapeDtypeStruct((size_x, lines * 8, LANES), F32),
+            jax.ShapeDtypeStruct((lines * 8, LANES), F32),
+        ),
+        in_specs=[pl.BlockSpec(memory_space=pltpu.MemorySpace.HBM)] * 5,
+        out_specs=(whole, whole),
+        scratch_shapes=[
+            pltpu.SMEM((block_count,), jnp.int32),
+            pltpu.SMEM((block_count,), jnp.int32),
+            vmem((10, slots), F32),
+            vmem((3, slots), F32),
+            vmem((3, slots), jnp.int32),
+            pltpu.SemaphoreType.DMA((5,)),
+            vmem((groups * TILE, LANES), F32),
+            vmem((256, LANES), F32),
+            vmem((ROWS, 6 * LANES), BF16),
+            vmem((NZ, 6 * LANES), BF16),
+            vmem((ROWS, 6 * LANES), BF16),
+            vmem((NZ, 6 * LANES), BF16),
+            vmem((2, lines * ROWS_Y, LANES), F32),
+            vmem((2, (lines + 1) * 4, LANES), F32),
+            vmem((BATCH, TILE, LANES), F32),
+            pltpu.SMEM((8,), jnp.int32),
+            pltpu.SMEM((block_count + 16,), jnp.int32),
+            pltpu.SMEM((block_count + 16,), jnp.int32),
+            pltpu.SMEM((block_count + 16,), jnp.int32),
+        ],
+        compiler_params=pltpu.CompilerParams(vmem_limit_bytes=20 << 20),
+        name="spread",
+    )
 
 
 def per_device(multipoles, fractions, base_index, block_plane, atom_count, coupling):
@@ -293,38 +437,16 @@
     cells_y = NY // size_y
     block_count = block_plane.shape[0]
     devices = size_x * size_y
-    lines = cells_x + 3
     (x_high, x_low), (y_high, y_low) = tables(size_x, size_y)
-    groups = block_count + 2 * (cells_x // XB) + 2
     vmem = pltpu.VMEM
-    smem = pl.BlockSpec(memory_space=pltpu.SMEM)
     whole = pl.BlockSpec(memory_space=pltpu.VMEM)
-    limit = pltpu.CompilerParams(vmem_limit_bytes=56 << 20)
-
-    density, rim = pl.pallas_call(
-        lambda *refs: spread_kernel(cells_x, cells_y, block_count, *refs),
-        out_shape=(
-            jax.ShapeDtypeStruct((size_x, lines * 8, LANES), F32),
-            jax.ShapeDtypeStruct((lines * 8, LANES), F32),
-        ),
-        in_specs=[smem, smem, whole, whole, whole],
-        out_specs=(whole, whole),
-        scratch_shapes=[
-            vmem((groups * TILE, LANES), F32),
-            vmem((256, LANES), F32),
-            vmem((WIN_X * ROWS_Y, 6 * LANES), BF16),
-            vmem((NZ, 6 * LANES), BF16),
-            vmem((WIN_X * ROWS_Y, 6 * LANES), BF16),
-            vmem((NZ, 6 * LANES), BF16),
-            vmem((2, lines * ROWS_Y, LANES), F32),
-            vmem((TILE, LANES), F32),
-            pltpu.SMEM((8,), jnp.int32),
-            pltpu.SMEM((block_count + 16,), jnp.int32),
-            pltpu.SMEM((block_count + 16,), jnp.int32),
-        ],
-        compiler_params=limit,
-        name="spread",
-    )(block_plane, atom_count, multipoles, fractions, base_index)
+    limit = pltpu.CompilerParams(vmem_limit_bytes=20 << 20)
+
+    hbm = pltpu.MemorySpace.HBM
+    atoms = (block_plane, atom_count, multipoles, fractions, base_index)
+    density, rim = make_spread(block_count, cells_x, cells_y, size_x)(
+        *[pltpu.with_memory_space_constraint(array, hbm) for array in atoms]
+    )
 
     rim = lax.ppermute(rim, "gy", [(i, (i + 1) % size_y) for i in range(size_y)])
     density = density.at[0].add(rim)
@@ -351,12 +473,12 @@
         grid=(MBLK,),
         in_specs=[
             pl.BlockSpec((devices * 32, LANES), fixed, pipeline_mode=pl.Buffered(1)),
-            pl.BlockSpec((NY, 2 * NY), fixed, pipeline_mode=pl.Buffered(1)),
-            pl.BlockSpec((NY, 2 * NY), fixed, pipeline_mode=pl.Buffered(1)),
+            pl.BlockSpec((2, NY // 2, NY), lambda i: (0, 0, 0), pipeline_mode=pl.Buffered(1)),
+            pl.BlockSpec((2, NY // 2, NY), lambda i: (0, 0, 0), pipeline_mode=pl.Buffered(1)),
             pl.BlockSpec((1, NZ, NZ), lambda i: (i, 0, 0)),
         ],
         out_specs=pl.BlockSpec((2, 2, NY // MBLK, NZ), lambda i: (0, 0, i, 0)),
-        scratch_shapes=[vmem((2 * NY, 4 * NZ), BF16), vmem((NY, 4 * NZ), F32)],
+        scratch_shapes=[vmem((2, NY, 4 * NZ), BF16), vmem((NY, 4 * NZ), BF16)],
         compiler_params=limit,
         name="transform_y",
     )(spectrum, jnp.asarray(y_high), jnp.asarray(y_low), coupling)

time: 129 us -> 106 us (0.82)
  Pallas kernels: 44.7 us -> 24 us
  blocking collectives: 75.8 us -> 73.1 us
  waiting for transfers between devices: 4.12 us -> 6.42 us
  other arithmetic: 1.58 us -> 0.03 us
    pallas_call x1, Pallas kernels: 28.4 us -> 15.5 us  [per_device(): make_spread(block_count, cells_x, cells_y, size_x)]
    pallas_call x1, Pallas kernels: 10.5 us -> 6.07 us  [per_device(): pl.pallas_call(y_kernel, out_shape=jax.ShapeDtypeStruct((2, 2, NY, NZ), F...]
    pallas_call x1, Pallas kernels: 5.72 us -> 2.52 us  [per_device(): pl.pallas_call(lambda *refs: x_kernel(size_x, cells_x, *refs), out_shape=...]
    ppermute x1, waiting for transfers between devices: 4.12 us -> 6.42 us  [per_device(): lax.ppermute(rim, 'gy', [(i, (i + 1) % size_y) for i in range(size_y)])]
    scatter-add x1, other arithmetic: 1.58 us -> 0.03 us  [per_device(): density = density.at[0].add(rim)]
    all_to_all x1, blocking collectives: 40.8 us -> 39.4 us  [per_device(): lax.all_to_all(density, 'gx', split_axis=0, concat_axis=0, tiled=True)]
    all_to_all x1, blocking collectives: 35 us -> 33.7 us  [per_device(): lax.all_to_all(spectrum.reshape(devices, 32, LANES), ('gx', 'gy'), split_...]
where the time goes in v2:
time: 106 us
  blocking collectives  73.1 us (69%)
  Pallas kernels  24 us (23%)
  waiting for transfers between devices  6.42 us (6%)
  starting transfers between devices  2.19 us (2%)
    all_to_all x1, blocking collectives, per_device(): lax.all_to_all(density, 'gx', split_axis=0, concat_axis=0, tiled=True)  39.4 us
    all_to_all x1, blocking collectives, per_device(): lax.all_to_all(spectrum.reshape(devices, 32, LANES), ('gx', 'gy'), split_...  33.7 us
    pallas_call x1, Pallas kernels, per_device(): make_spread(block_count, cells_x, cells_y, size_x)  15.5 us
    ppermute x1, waiting for transfers between devices, per_device(): lax.ppermute(rim, 'gy', [(i, (i + 1) % size_y) for i in range(size_y)])  6.42 us
    pallas_call x1, Pallas kernels, per_device(): pl.pallas_call(y_kernel, out_shape=jax.ShapeDtypeStruct((2, 2, NY, NZ), F...  6.07 us
    pallas_call x1, Pallas kernels, per_device(): pl.pallas_call(lambda *refs: x_kernel(size_x, cells_x, *refs), out_shape=...  2.52 us
    ppermute x1, starting transfers between devices, per_device(): lax.ppermute(rim, 'gy', [(i, (i + 1) % size_y) for i in range(size_y)])  2.19 us
  transfers between devices with their start and end apart: 1, of which 1 were waited for; matrix products, arithmetic and copies ran while one was open for 0% of the time, Pallas kernels for 0%

profile of v2, /device:TPU:1, one launch (start us, length us, event | category | flops | bytes accessed | tf_op | source)
XLA Modules:
  0.0 105.9 jit_solution(7954775199635965512)
XLA Ops:
  0.0 15.5 %spread.1 = (f32[16,280,128]{2,1,0:T(8,128)S(1)}, f32[280,128]{1,0:T(8,128)S(1)}) custom-call(s32[64]{0:T(128)} %refs_0_.1, s32[64]{0:T(128)} %refs_1_.2, f32[10,8192]{1,0:T(8,128)} %refs_2_.2, f32[3,8192]{1,0:T(4,128)} %refs_3_.1, s32[3,8192]{1,0:T(4,128)} %refs_4_.1), custom_call_target="tpu_custom_call" | custom-call | tf_op jit(solution)/shard_map/spread/pallas_call | solution.py:447
  15.5 2.2 %collective-permute-start = (f32[280,128]{1,0:T(8,128)S(1)}, f32[280,128]{1,0:T(8,128)S(1)}, u32[]{:S(2)}, u32[]{:S(2)}) collective-permute-start(f32[280,128]{1,0:T(8,128)S(1)} %get-tuple-element.20), channel_id=1, source_target_pairs={{0,1},{1,2},{2,3},{3,4},{4,5},{5,6},{6,7},{7,0},{8,9},{9,10},{10,1... | collective-permute-start | bytes 430088 | tf_op jit(solution)/shard_map/ppermute | solution.py:451
  17.7 6.4 %collective-permute-done = f32[280,128]{1,0:T(8,128)S(1)} collective-permute-done((f32[280,128]{1,0:T(8,128)S(1)}, f32[280,128]{1,0:T(8,128)S(1)}, u32[]{:S(2)}, u32[]{:S(2)}) %collective-permute-start) | collective-permute-done | bytes 143392 | tf_op jit(solution)/shard_map/ppermute | solution.py:451
  24.1 0.0 copy-start.3
  24.1 0.0 copy-start.4
  24.1 39.4 %all_to_all.10.refs_0_ = f32[16,280,128]{2,1,0:T(8,128)S(1)} all-to-all(f32[16,280,128]{2,1,0:T(8,128)S(1)} %fusion), channel_id=1, replica_groups=mesh['gx'=16,'gy'=8] {'gx'}, dimensions={0} | all-to-all | bytes 4587520 | tf_op jit(solution)/shard_map/all_to_all | solution.py:453
  63.6 0.0 copy-done.3
  63.6 0.0 copy-done.4
  63.6 2.5 %transform_x.1 = f32[4096,128]{1,0:T(8,128)S(1)} custom-call(f32[16,280,128]{2,1,0:T(8,128)S(1)} %all_to_all.10.refs_0_, bf16[512,512]{1,0:T(8,128)(2,1)S(1)} %copy-done.4, bf16[512,512]{1,0:T(8,128)(2,1)S(1)} %copy-done.3), custom_call_target="tpu_custom_call" | custom-call | tf_op jit(solution)/shard_map/transform_x/pallas_call | solution.py:455
  66.1 0.0 copy-start
  66.1 0.0 copy-start.1
  66.1 0.0 copy-start.2
  66.1 33.7 %all_to_all.11 = f32[128,32,128]{2,1,0:T(8,128)S(1)} all-to-all(f32[128,32,128]{2,1,0:T(8,128)S(1)} %bitcast.7), channel_id=1, replica_groups=mesh['gx'=16,'gy'=8] {'gx','gy'}, dimensions={0} | all-to-all | bytes 4194304 | tf_op jit(solution)/shard_map/all_to_all | solution.py:465
  99.8 0.0 copy-done
  99.8 0.0 copy-done.1
  99.8 0.0 copy-done.2
  99.9 6.1 %transform_y.1 = f32[2,2,512,256]{3,2,1,0:T(8,128)} custom-call(f32[4096,128]{1,0:T(8,128)S(1)} %bitcast.6, bf16[2,256,512]{2,1,0:T(8,128)(2,1)S(1)} %copy-done.2, bf16[2,256,512]{2,1,0:T(8,128)(2,1)S(1)} %copy-done.1, f32[8,256,256]{2,1,0:T(8,128)S(1)} %copy-done), custom_call_target="tpu_custom_call" | custom-call | tf_op jit(solution)/shard_map/transform_y/pallas_call | solution.py:470
  (1 shorter events, 0.0 us)
Async XLA Ops:
  15.5 8.6 %collective-permute-start = (f32[280,128]{1,0:T(8,128)S(1)}, f32[280,128]{1,0:T(8,128)S(1)}, u32[]{:S(2)}, u32[]{:S(2)}) collective-permute-start(f32[280,128]{1,0:T(8,128)S(1)} %get-tuple-element.20), channel_id=1, source_target_pairs={{0,1},{1,2},{2,3},{3,4},{4,5},{5,6},{6,7},{7,0},{8,9},{9,10},{10,1... | collective-permute-start | bytes 430088 | tf_op jit(solution)/shard_map/ppermute | solution.py:451
  24.1 39.5 %copy-start.3 = (bf16[512,512]{1,0:T(8,128)(2,1)S(1)}, bf16[512,512]{1,0:T(8,128)(2,1)}, u32[]{:S(2)}) copy-start(bf16[512,512]{1,0:T(8,128)(2,1)} %constant.36.clone.refs_2_) | copy-start | bytes 1572868
  24.1 39.4 %copy-start.4 = (bf16[512,512]{1,0:T(8,128)(2,1)S(1)}, bf16[512,512]{1,0:T(8,128)(2,1)}, u32[]{:S(2)}) copy-start(bf16[512,512]{1,0:T(8,128)(2,1)} %constant.35.clone.refs_1_) | copy-start | bytes 1572868
  66.1 33.8 %copy-start = (f32[8,256,256]{2,1,0:T(8,128)S(1)}, f32[8,256,256]{2,1,0:T(8,128)}, u32[]{:S(2)}) copy-start(f32[8,256,256]{2,1,0:T(8,128)} %coupling_ref.1) | copy-start | bytes 6291460
  66.1 33.7 %copy-start.1 = (bf16[2,256,512]{2,1,0:T(8,128)(2,1)S(1)}, bf16[2,256,512]{2,1,0:T(8,128)(2,1)}, u32[]{:S(2)}) copy-start(bf16[2,256,512]{2,1,0:T(8,128)(2,1)} %constant.38.clone.low_ref) | copy-start | bytes 1572868
  66.1 33.7 %copy-start.2 = (bf16[2,256,512]{2,1,0:T(8,128)(2,1)S(1)}, bf16[2,256,512]{2,1,0:T(8,128)(2,1)}, u32[]{:S(2)}) copy-start(bf16[2,256,512]{2,1,0:T(8,128)(2,1)} %constant.37.clone.high_ref) | copy-start | bytes 1572868

commit v3 on v2

--- a/solution.py
+++ b/solution.py
@@ -48,8 +48,8 @@
     return ((w3 * u + w2) * u + w1) * u + w0, (d2 * u + d1) * u + d0, s1 * u + s0
 
 
-def spread_kernel(cells_x, cells_y, block_count, plane_in, count_in, moment_in, fraction_in, base_in, out_ref, rim_ref,
-                  plane_ref, count_ref, moment_ref, fraction_ref, base_ref, arrived, raw, taps, a0, b0, a1, b1, density, edge, stage, cursor, pair_group, pair_plane, pair_last):
+def spread_kernel(cells_x, cells_y, block_count, plane_in, count_in, moment_in, fraction_in, base_in, density, rim_ref,
+                  plane_ref, count_ref, moment_ref, fraction_ref, base_ref, arrived, raw, taps, a0, b0, a1, b1, edge, stage, cursor, pair_group, pair_plane, pair_last):
     planes = cells_x // XB
     spare = block_count + 2 * planes
     lane = lax.broadcasted_iota(jnp.int32, (TILE, LANES), 1)
@@ -191,6 +191,16 @@
                         value = jnp.where(hit[c], ztap[k][c], value)
                     b_ref[TILE * t:TILE * (t + 1), (member * 3 + k) * LANES:(member * 3 + k + 1) * LANES] = value
                 yield
+
+        for member in range(2):
+            base = (pair_group[q] + member) * TILE
+            first = (slot * 2 + member) * 64
+
+            def wide(r, base=base):
+                return raw[pl.ds(base + r, TILE, stride=0), :].astype(BF16)
+
+            def tap(r, first=first):
+                return taps[pl.ds(first + r, TILE, stride=0), :].astype(BF16)
 
             ybase = wide(14)
             xbase = wide(13)
@@ -237,25 +247,22 @@
                               (member * 3 + k) * LANES:(member * 3 + k + 1) * LANES] = column[x]
                     yield
 
+    def push(b_ref, part, unit, register):
+        cut = slice(part * 2 * LANES, (part + 1) * 2 * LANES)
+        pltpu.matmul_push_rhs(b_ref[:, cut], register, unit, transpose=True)
+
     def multiply(sums, a_ref, b_ref):
-        def push(part, unit, register):
-            cut = slice(part * 2 * LANES, (part + 1) * 2 * LANES)
-            pltpu.matmul_push_rhs(b_ref[:, cut], register, unit, transpose=True)
-
         def add(part, unit, i, register):
             row, size = CHUNKS[i]
             lhs = a_ref[row:row + size, part * 2 * LANES:(part + 1) * 2 * LANES]
             pltpu.matmul_acc_lhs(sums[unit * len(CHUNKS) + i], lhs, load_staged_rhs=register)
 
-        push(0, 0, 0)
-        push(1, 1, 0)
-        yield
         for i in range(len(CHUNKS)):
             for unit in range(2):
                 add(unit, unit, i, None if i else 0)
                 yield
             if i < 2:
-                push(2, i, 1)
+                push(b_ref, 2, i, 1)
         for i in range(len(CHUNKS) // 2):
             for unit in range(2):
                 add(2, unit, i + unit * (len(CHUNKS) // 2), None if i else 1)
@@ -277,8 +284,10 @@
 
     def step(sums, q, now, later, slot):
         steps = multiply(sums, *now)
+        for unit in range(2):
+            push(now[1], unit, unit, 0)
         for i, _ in enumerate(build(q + 1, *later, slot)):
-            if i % BUILD_STEPS == 0:
+            if i >= 2 * BUILD_STEPS and i % BUILD_STEPS == 0:
                 next(steps, None)
         for _ in steps:
             pass
@@ -301,17 +310,23 @@
     pl.run_scoped(turns, *[pltpu.ACC(unit)((size, NZ), F32) for unit in range(2) for _, size in CHUNKS])
 
     lines = cells_x + 3
-    width = out_ref.shape[1] // lines
-    columns = width // 2
+    width = rim_ref.shape[0] // lines
     for half in range(2):
-        for y in range(cells_y):
-            out_ref[y // columns, pl.ds(y % columns * 2 + half, lines, stride=width), :] = (
-                density.at[half][pl.ds(y, lines, stride=ROWS_Y), :]
-            )
         for y in range(3):
             rim_ref[pl.ds(y * 2 + half, lines, stride=width), :] = edge.at[half][pl.ds(y, lines, stride=4), :]
     for r in range(6, width):
         rim_ref[pl.ds(r, lines, stride=width), :] = jnp.zeros((lines, LANES), F32)
+
+
+def line_kernel(density_ref, out_ref):
+    lines = density_ref.shape[1] // ROWS_Y
+    width = out_ref.shape[1] // lines
+    columns = width // 2
+    for half in range(2):
+        for y in range(ROWS_Y):
+            out_ref[y // columns, pl.ds(y % columns * 2 + half, lines, stride=width), :] = (
+                density_ref.at[half][pl.ds(y, lines, stride=ROWS_Y), :]
+            )
 
 
 def x_kernel(groups, cells_x, in_ref, high_ref, low_ref, out_ref, lines, narrow):
@@ -334,7 +349,7 @@
             )
 
 
-def y_kernel(in_ref, high_ref, low_ref, coupling_ref, out_ref, data, spectrum):
+def y_kernel(per_step, in_ref, high_ref, low_ref, coupling_ref, out_ref, data, spectrum):
     @pl.when(pl.program_id(0) == 0)
     def _():
         half_y = NY // 2
@@ -357,17 +372,19 @@
         spectrum[half_y:NY, :] = (even - odd).astype(BF16)
 
     block = NY // MBLK
-    rows = spectrum[pl.ds(pl.multiple_of(pl.program_id(0) * block, block), block), :]
-    rows = jnp.concatenate([rows[:, q * NZ:(q + 1) * NZ] for q in range(4)], axis=0)
-    weight = coupling_ref[0]
-    high = weight.astype(BF16)
-    low = (weight - high.astype(F32)).astype(BF16)
     dims = (((1,), (1,)), ((), ()))
-    result = lax.dot_general(rows, high, dims, preferred_element_type=F32) + lax.dot_general(
-        rows, low, dims, preferred_element_type=F32
-    )
-    for q in range(4):
-        out_ref[q % 2, q // 2, :, :] = result[q * block:(q + 1) * block]
+    for member in range(per_step):
+        first = (pl.program_id(0) * per_step + member) * block
+        rows = spectrum[pl.ds(pl.multiple_of(first, block), block), :]
+        rows = jnp.concatenate([rows[:, q * NZ:(q + 1) * NZ] for q in range(4)], axis=0)
+        weight = coupling_ref[member]
+        high = weight.astype(BF16)
+        low = (weight - high.astype(F32)).astype(BF16)
+        result = lax.dot_general(rows, high, dims, preferred_element_type=F32) + lax.dot_general(
+            rows, low, dims, preferred_element_type=F32
+        )
+        for q in range(4):
+            out_ref[q % 2, q // 2, member * block:(member + 1) * block, :] = result[q * block:(q + 1) * block]
 
 
 def two_parts(table):
@@ -399,7 +416,7 @@
     return pl.pallas_call(
         lambda *refs: spread_kernel(cells_x, cells_y, block_count, *refs),
         out_shape=(
-            jax.ShapeDtypeStruct((size_x, lines * 8, LANES), F32),
+            jax.ShapeDtypeStruct((2, lines * ROWS_Y, LANES), F32),
             jax.ShapeDtypeStruct((lines * 8, LANES), F32),
         ),
         in_specs=[pl.BlockSpec(memory_space=pltpu.MemorySpace.HBM)] * 5,
@@ -417,7 +434,6 @@
             vmem((NZ, 6 * LANES), BF16),
             vmem((ROWS, 6 * LANES), BF16),
             vmem((NZ, 6 * LANES), BF16),
-            vmem((2, lines * ROWS_Y, LANES), F32),
             vmem((2, (lines + 1) * 4, LANES), F32),
             vmem((BATCH, TILE, LANES), F32),
             pltpu.SMEM((8,), jnp.int32),
@@ -430,6 +446,29 @@
     )
 
 
+def make_y(size_x, size_y, per_step):
+    devices = size_x * size_y
+    _, (y_high, y_low) = tables(size_x, size_y)
+    vmem = pltpu.VMEM
+    fixed = lambda i: (0, 0)
+    call = pl.pallas_call(
+        lambda *refs: y_kernel(per_step, *refs),
+        out_shape=jax.ShapeDtypeStruct((2, 2, NY, NZ), F32),
+        grid=(MBLK // per_step,),
+        in_specs=[
+            pl.BlockSpec((devices * 32, LANES), fixed, pipeline_mode=pl.Buffered(1)),
+            pl.BlockSpec((2, NY // 2, NY), lambda i: (0, 0, 0), pipeline_mode=pl.Buffered(1)),
+            pl.BlockSpec((2, NY // 2, NY), lambda i: (0, 0, 0), pipeline_mode=pl.Buffered(1)),
+            pl.BlockSpec((per_step, NZ, NZ), lambda i: (i, 0, 0)),
+        ],
+        out_specs=pl.BlockSpec((2, 2, NY // MBLK * per_step, NZ), lambda i: (0, 0, i, 0)),
+        scratch_shapes=[vmem((2, NY, 4 * NZ), BF16), vmem((NY, 4 * NZ), BF16)],
+        compiler_params=pltpu.CompilerParams(vmem_limit_bytes=20 << 20),
+        name="transform_y",
+    )
+    return lambda spectrum, coupling: call(spectrum, jnp.asarray(y_high), jnp.asarray(y_low), coupling)
+
+
 def per_device(multipoles, fractions, base_index, block_plane, atom_count, coupling):
     size_x = lax.axis_size("gx")
     size_y = lax.axis_size("gy")
@@ -437,7 +476,7 @@
     cells_y = NY // size_y
     block_count = block_plane.shape[0]
     devices = size_x * size_y
-    (x_high, x_low), (y_high, y_low) = tables(size_x, size_y)
+    (x_high, x_low), _ = tables(size_x, size_y)
     vmem = pltpu.VMEM
     whole = pl.BlockSpec(memory_space=pltpu.VMEM)
     limit = pltpu.CompilerParams(vmem_limit_bytes=20 << 20)
@@ -449,6 +488,14 @@
     )
 
     rim = lax.ppermute(rim, "gy", [(i, (i + 1) % size_y) for i in range(size_y)])
+    density = pl.pallas_call(
+        line_kernel,
+        out_shape=jax.ShapeDtypeStruct((size_x, (cells_x + 3) * 8, LANES), F32),
+        in_specs=[whole],
+        out_specs=whole,
+        compiler_params=limit,
+        name="lines",
+    )(density)
     density = density.at[0].add(rim)
     density = lax.all_to_all(density, "gx", split_axis=0, concat_axis=0, tiled=True)
 
@@ -466,22 +513,7 @@
         spectrum.reshape(devices, 32, LANES), ("gx", "gy"), split_axis=0, concat_axis=0, tiled=True
     ).reshape(devices * 32, LANES)
 
-    fixed = lambda i: (0, 0)
-    return pl.pallas_call(
-        y_kernel,
-        out_shape=jax.ShapeDtypeStruct((2, 2, NY, NZ), F32),
-        grid=(MBLK,),
-        in_specs=[
-            pl.BlockSpec((devices * 32, LANES), fixed, pipeline_mode=pl.Buffered(1)),
-            pl.BlockSpec((2, NY // 2, NY), lambda i: (0, 0, 0), pipeline_mode=pl.Buffered(1)),
-            pl.BlockSpec((2, NY // 2, NY), lambda i: (0, 0, 0), pipeline_mode=pl.Buffered(1)),
-            pl.BlockSpec((1, NZ, NZ), lambda i: (i, 0, 0)),
-        ],
-        out_specs=pl.BlockSpec((2, 2, NY // MBLK, NZ), lambda i: (0, 0, i, 0)),
-        scratch_shapes=[vmem((2, NY, 4 * NZ), BF16), vmem((NY, 4 * NZ), BF16)],
-        compiler_params=limit,
-        name="transform_y",
-    )(spectrum, jnp.asarray(y_high), jnp.asarray(y_low), coupling)
+    return make_y(size_x, size_y, 4)(spectrum, coupling)
 
 
 def solution(mesh):

time: 106 us -> 103 us (0.972)
  waiting for transfers between devices: 6.42 us -> 3.76 us
  Pallas kernels: 24 us -> 22.2 us
  starting transfers between devices: 2.19 us -> 3.33 us
    ppermute x1, waiting for transfers between devices: 6.42 us -> 3.76 us  [per_device(): lax.ppermute(rim, 'gy', [(i, (i + 1) % size_y) for i in range(size_y)])]
    pallas_call x1, Pallas kernels: 15.5 us -> 14.3 us  [per_device(): make_spread(block_count, cells_x, cells_y, size_x)]
    ppermute x1, starting transfers between devices: 2.19 us -> 3.33 us  [per_device(): lax.ppermute(rim, 'gy', [(i, (i + 1) % size_y) for i in range(size_y)])]
    pallas_call x1 -> x2, Pallas kernels: 6.07 us -> 5.35 us  [the longest x1 3.86 us: make_y(): call(spectrum, jnp.asarray(y_high), jnp.asarray(y_low), coupling)]
  transfers between devices with their start and end apart: 1 -> 1, of which waited for: 1 -> 1; matrix products, arithmetic and copies ran while one was open for 0% -> 0% of each run, Pallas kernels for 0% -> 1%
where the time goes in v3:
time: 103 us
  blocking collectives  73.2 us (71%)
  Pallas kernels  22.2 us (22%)
  waiting for transfers between devices  3.76 us (4%)
  starting transfers between devices  3.33 us (3%)
    all_to_all x1, blocking collectives, per_device(): lax.all_to_all(density, 'gx', split_axis=0, concat_axis=0, tiled=True)  39.5 us
    all_to_all x1, blocking collectives, per_device(): lax.all_to_all(spectrum.reshape(devices, 32, LANES), ('gx', 'gy'), split_...  33.7 us
    pallas_call x1, Pallas kernels, per_device(): make_spread(block_count, cells_x, cells_y, size_x)  14.3 us
    pallas_call x1, Pallas kernels, make_y(): call(spectrum, jnp.asarray(y_high), jnp.asarray(y_low), coupling)  3.86 us
    ppermute x1, waiting for transfers between devices, per_device(): lax.ppermute(rim, 'gy', [(i, (i + 1) % size_y) for i in range(size_y)])  3.76 us
    ppermute x1, starting transfers between devices, per_device(): lax.ppermute(rim, 'gy', [(i, (i + 1) % size_y) for i in range(size_y)])  3.33 us
    pallas_call x1, Pallas kernels, per_device(): pl.pallas_call(lambda *refs: x_kernel(size_x, cells_x, *refs), out_shape=...  2.51 us
  transfers between devices with their start and end apart: 1, of which 1 were waited for; matrix products, arithmetic and copies ran while one was open for 0% of the time, Pallas kernels for 1%

profile of v3, /device:TPU:1, one launch (start us, length us, event | category | flops | bytes accessed | tf_op | source)
XLA Modules:
  0.0 102.6 jit_solution(17708315781569949231)
XLA Ops:
  0.0 14.3 %spread.1 = (f32[2,2240,128]{2,1,0:T(8,128)S(1)}, f32[280,128]{1,0:T(8,128)S(1)}) custom-call(s32[64]{0:T(128)} %refs_0_.1, s32[64]{0:T(128)} %refs_1_.3, f32[10,8192]{1,0:T(8,128)} %refs_2_.3, f32[3,8192]{1,0:T(4,128)} %refs_3_.2, s32[3,8192]{1,0:T(4,128)} %refs_4_.1), custom_call_target="tpu_custom_call" | custom-call | tf_op jit(solution)/shard_map/spread/pallas_call | solution.py:486
  14.3 3.3 %collective-permute-start = (f32[280,128]{1,0:T(8,128)S(1)}, f32[280,128]{1,0:T(8,128)S(1)}, u32[]{:S(2)}, u32[]{:S(2)}) collective-permute-start(f32[280,128]{1,0:T(8,128)S(1)} %get-tuple-element.20), channel_id=1, source_target_pairs={{0,1},{1,2},{2,3},{3,4},{4,5},{5,6},{6,7},{7,0},{8,9},{9,10},{10,1... | collective-permute-start | bytes 430088 | tf_op jit(solution)/shard_map/ppermute | solution.py:490
  17.6 1.5 %lines.1 = f32[16,280,128]{2,1,0:T(8,128)S(1)} custom-call(f32[2,2240,128]{2,1,0:T(8,128)S(1)} %get-tuple-element.19.density_ref), custom_call_target="tpu_custom_call" | custom-call | tf_op jit(solution)/shard_map/lines/pallas_call | solution.py:491
  19.1 3.8 %collective-permute-done = f32[280,128]{1,0:T(8,128)S(1)} collective-permute-done((f32[280,128]{1,0:T(8,128)S(1)}, f32[280,128]{1,0:T(8,128)S(1)}, u32[]{:S(2)}, u32[]{:S(2)}) %collective-permute-start) | collective-permute-done | bytes 143392 | tf_op jit(solution)/shard_map/ppermute | solution.py:490
  22.9 0.0 copy-start.3
  22.9 0.0 copy-start.4
  23.0 39.5 %all_to_all.10.refs_0_ = f32[16,280,128]{2,1,0:T(8,128)S(1)} all-to-all(f32[16,280,128]{2,1,0:T(8,128)S(1)} %fusion), channel_id=1, replica_groups=mesh['gx'=16,'gy'=8] {'gx'}, dimensions={0} | all-to-all | bytes 4587520 | tf_op jit(solution)/shard_map/all_to_all | solution.py:500
  62.5 0.0 copy-done.3
  62.5 0.0 copy-done.4
  62.5 2.5 %transform_x.1 = f32[4096,128]{1,0:T(8,128)S(1)} custom-call(f32[16,280,128]{2,1,0:T(8,128)S(1)} %all_to_all.10.refs_0_, bf16[512,512]{1,0:T(8,128)(2,1)S(1)} %copy-done.4, bf16[512,512]{1,0:T(8,128)(2,1)S(1)} %copy-done.3), custom_call_target="tpu_custom_call" | custom-call | tf_op jit(solution)/shard_map/transform_x/pallas_call | solution.py:502
  65.0 0.0 copy-start
  65.0 0.0 copy-start.1
  65.0 0.0 copy-start.2
  65.0 33.7 %all_to_all.11 = f32[128,32,128]{2,1,0:T(8,128)S(1)} all-to-all(f32[128,32,128]{2,1,0:T(8,128)S(1)} %bitcast.5), channel_id=1, replica_groups=mesh['gx'=16,'gy'=8] {'gx','gy'}, dimensions={0} | all-to-all | bytes 4194304 | tf_op jit(solution)/shard_map/all_to_all | solution.py:512
  98.7 0.0 copy-done
  98.7 0.0 copy-done.1
  98.7 0.0 copy-done.2
  98.7 3.9 %transform_y.1 = f32[2,2,512,256]{3,2,1,0:T(8,128)} custom-call(f32[4096,128]{1,0:T(8,128)S(1)} %bitcast.4, bf16[2,256,512]{2,1,0:T(8,128)(2,1)S(1)} %copy-done.2, bf16[2,256,512]{2,1,0:T(8,128)(2,1)S(1)} %copy-done.1, f32[8,256,256]{2,1,0:T(8,128)S(1)} %copy-done), custom_call_target="tpu_custom_call" | custom-call | tf_op jit(solution)/shard_map/transform_y/pallas_call | solution.py:469
  (1 shorter events, 0.0 us)
Async XLA Ops:
  14.3 8.6 %collective-permute-start = (f32[280,128]{1,0:T(8,128)S(1)}, f32[280,128]{1,0:T(8,128)S(1)}, u32[]{:S(2)}, u32[]{:S(2)}) collective-permute-start(f32[280,128]{1,0:T(8,128)S(1)} %get-tuple-element.20), channel_id=1, source_target_pairs={{0,1},{1,2},{2,3},{3,4},{4,5},{5,6},{6,7},{7,0},{8,9},{9,10},{10,1... | collective-permute-start | bytes 430088 | tf_op jit(solution)/shard_map/ppermute | solution.py:490
  22.9 39.5 %copy-start.3 = (bf16[512,512]{1,0:T(8,128)(2,1)S(1)}, bf16[512,512]{1,0:T(8,128)(2,1)}, u32[]{:S(2)}) copy-start(bf16[512,512]{1,0:T(8,128)(2,1)} %constant.36.clone.refs_2_) | copy-start | bytes 1572868
  22.9 39.5 %copy-start.4 = (bf16[512,512]{1,0:T(8,128)(2,1)S(1)}, bf16[512,512]{1,0:T(8,128)(2,1)}, u32[]{:S(2)}) copy-start(bf16[512,512]{1,0:T(8,128)(2,1)} %constant.35.clone.refs_1_) | copy-start | bytes 1572868
  65.0 33.8 %copy-start = (f32[8,256,256]{2,1,0:T(8,128)S(1)}, f32[8,256,256]{2,1,0:T(8,128)}, u32[]{:S(2)}) copy-start(f32[8,256,256]{2,1,0:T(8,128)} %refs_3_.3) | copy-start | bytes 6291460
  65.0 33.7 %copy-start.1 = (bf16[2,256,512]{2,1,0:T(8,128)(2,1)S(1)}, bf16[2,256,512]{2,1,0:T(8,128)(2,1)}, u32[]{:S(2)}) copy-start(bf16[2,256,512]{2,1,0:T(8,128)(2,1)} %constant.38.clone.refs_2_) | copy-start | bytes 1572868
  65.0 33.7 %copy-start.2 = (bf16[2,256,512]{2,1,0:T(8,128)(2,1)S(1)}, bf16[2,256,512]{2,1,0:T(8,128)(2,1)}, u32[]{:S(2)}) copy-start(bf16[2,256,512]{2,1,0:T(8,128)(2,1)} %constant.37.clone.refs_1_) | copy-start | bytes 1572868

commit v4 on v3

--- a/solution.py
+++ b/solution.py
@@ -51,7 +51,8 @@
 def spread_kernel(cells_x, cells_y, block_count, plane_in, count_in, moment_in, fraction_in, base_in, density, rim_ref,
                   plane_ref, count_ref, moment_ref, fraction_ref, base_ref, arrived, raw, taps, a0, b0, a1, b1, edge, stage, cursor, pair_group, pair_plane, pair_last):
     planes = cells_x // XB
-    spare = block_count + 2 * planes
+    room = block_count + 2
+    spare = planes * room
     lane = lax.broadcasted_iota(jnp.int32, (TILE, LANES), 1)
 
     copies = [
@@ -74,38 +75,10 @@
     copies[0].wait()
     copies[1].wait()
 
+    zero_group = jnp.zeros((TILE, LANES), F32)
     for p in range(planes):
-        cursor[p] = 0
-
-    def tally(g, carry):
-        p = plane_ref[g]
-        cursor[p] = cursor[p] + count_ref[g]
-        return carry
-
-    lax.fori_loop(0, block_count, tally, 0)
-    zero_group = jnp.zeros((TILE, LANES), F32)
-    start = jnp.int32(0)
-    pairs = jnp.int32(0)
-    for p in range(planes):
-        total = cursor[p]
-        whole = (total + LANES - 1) // LANES
-        cursor[p] = start * LANES
-        raw[pl.ds(pl.multiple_of(start * TILE, TILE), TILE), :] = zero_group
-        here = (whole + 1) // 2
-
-        def note(i, carry, start=start, pairs=pairs, here=here, p=p):
-            pair_group[pairs + i] = start + 2 * i
-            pair_plane[pairs + i] = p
-            pair_last[pairs + i] = jnp.where(i == here - 1, 1, 0)
-            return carry
-
-        lax.fori_loop(0, here, note, 0)
-        pairs = pairs + here
-        start = start + total // LANES + 2
-    for i in range(3):
-        pair_group[pairs + i] = spare
-        pair_plane[pairs + i] = 0
-        pair_last[pairs + i] = 1
+        cursor[p] = p * room * LANES
+        raw[p * room * TILE:(p * room + 1) * TILE, :] = zero_group
     for i in range(2):
         raw[(spare + i) * TILE:(spare + i + 1) * TILE, :] = zero_group
 
@@ -135,9 +108,25 @@
         return carry
 
     lax.fori_loop(0, block_count // BATCH, append, 0)
+    pairs = jnp.int32(0)
     for p in range(planes):
+        start = p * room
         after = (cursor[p] + LANES - 1) // LANES
         raw[pl.ds(pl.multiple_of(after * TILE, TILE), TILE), :] = zero_group
+        here = (after - start + 1) // 2
+
+        def note(i, carry, start=start, pairs=pairs, here=here, p=p):
+            pair_group[pairs + i] = start + 2 * i
+            pair_plane[pairs + i] = p
+            pair_last[pairs + i] = jnp.where(i == here - 1, 1, 0)
+            return carry
+
+        lax.fori_loop(0, here, note, 0)
+        pairs = pairs + here
+    for i in range(3):
+        pair_group[pairs + i] = spare
+        pair_plane[pairs + i] = 0
+        pair_last[pairs + i] = 1
 
     sub = lax.broadcasted_iota(jnp.int32, (8, LANES), 0)
     inner = tap_constants(sub % 4)
@@ -329,18 +318,21 @@
             )
 
 
-def x_kernel(groups, cells_x, in_ref, high_ref, low_ref, out_ref, lines, narrow):
+def x_kernel(groups, cells_x, in_ref, table_ref, out_ref, narrow):
     width = 8
+    spilled = lax.broadcasted_iota(jnp.int32, (8, LANES), 0) < 3
     for l in range(width):
         cut = slice(l * LANES, (l + 1) * LANES)
         for src in range(groups):
-            lines[src * cells_x:(src + 1) * cells_x, cut] = in_ref[src, pl.ds(l, cells_x, stride=width), :]
-        for src in range(groups):
-            first = (src + 1) % groups * cells_x
-            lines[first:first + 3, cut] = lines[first:first + 3, cut] + in_ref[src, pl.ds(cells_x * width + l, 3, stride=width), :]
-    narrow[...] = lines[...].astype(BF16)
+            own = in_ref[src, pl.ds(l, cells_x, stride=width), :]
+            last = in_ref[(src - 1) % groups, pl.ds((cells_x - 5) * width + l, 8, stride=width), :]
+            spill = jnp.where(spilled, pltpu.roll(last, 3, axis=0), 0.0)
+            narrow[src * cells_x:(src + 1) * cells_x, cut] = jnp.concatenate([own[:8] + spill, own[8:]], 0).astype(BF16)
+    half = table_ref.shape[0] // 2
     data = narrow[...]
-    result = jnp.dot(high_ref[...], data, preferred_element_type=F32) + jnp.dot(low_ref[...], data, preferred_element_type=F32)
+    result = jnp.dot(table_ref[:half], data, preferred_element_type=F32) + jnp.dot(
+        table_ref[half:], data, preferred_element_type=F32
+    )
     devices = out_ref.shape[0] // 32
     for q in range(4):
         for l in range(width):
@@ -349,7 +341,7 @@
             )
 
 
-def y_kernel(per_step, in_ref, high_ref, low_ref, coupling_ref, out_ref, data, spectrum):
+def y_kernel(per_step, in_ref, table_ref, coupling_ref, out_ref, data, spectrum):
     @pl.when(pl.program_id(0) == 0)
     def _():
         half_y = NY // 2
@@ -362,11 +354,7 @@
                     swap = slice((q ^ 1) * NZ + half * LANES, (q ^ 1) * NZ + (half + 1) * LANES)
                     data[odd, 0:half_y, same] = value.astype(BF16)
                     data[odd, half_y:NY, swap] = (value if q % 2 else -value).astype(BF16)
-            lines = data[odd]
-            sums.append(
-                jnp.dot(high_ref[odd], lines, preferred_element_type=F32)
-                + jnp.dot(low_ref[odd], lines, preferred_element_type=F32)
-            )
+            sums.append(split_dot(table_ref[odd], data[odd]))
         even, odd = sums
         spectrum[0:half_y, :] = (even + odd).astype(BF16)
         spectrum[half_y:NY, :] = (even - odd).astype(BF16)
@@ -390,7 +378,13 @@
 def two_parts(table):
     high = table.astype(ml_dtypes.bfloat16)
     low = (table - high.astype(np.float64)).astype(ml_dtypes.bfloat16)
-    return high, low
+    return np.concatenate([high, low], axis=-2)
+
+
+def split_dot(table, data):
+    both = jnp.dot(table, data, preferred_element_type=F32)
+    rows = both.shape[0] // 2
+    return both[:rows] + both[rows:]
 
 
 def tables(size_x, size_y):
@@ -409,7 +403,7 @@
 
 def make_spread(block_count, cells_x, cells_y, size_x):
     lines = cells_x + 3
-    groups = block_count + 2 * (cells_x // XB) + 2
+    groups = (block_count + 2) * (cells_x // XB) + 2
     vmem = pltpu.VMEM
     slots = block_count * LANES
     whole = pl.BlockSpec(memory_space=pltpu.VMEM)
@@ -448,7 +442,7 @@
 
 def make_y(size_x, size_y, per_step):
     devices = size_x * size_y
-    _, (y_high, y_low) = tables(size_x, size_y)
+    _, table = tables(size_x, size_y)
     vmem = pltpu.VMEM
     fixed = lambda i: (0, 0)
     call = pl.pallas_call(
@@ -457,8 +451,7 @@
         grid=(MBLK // per_step,),
         in_specs=[
             pl.BlockSpec((devices * 32, LANES), fixed, pipeline_mode=pl.Buffered(1)),
-            pl.BlockSpec((2, NY // 2, NY), lambda i: (0, 0, 0), pipeline_mode=pl.Buffered(1)),
-            pl.BlockSpec((2, NY // 2, NY), lambda i: (0, 0, 0), pipeline_mode=pl.Buffered(1)),
+            pl.BlockSpec((2, NY, NY), lambda i: (0, 0, 0), pipeline_mode=pl.Buffered(1)),
             pl.BlockSpec((per_step, NZ, NZ), lambda i: (i, 0, 0)),
         ],
         out_specs=pl.BlockSpec((2, 2, NY // MBLK * per_step, NZ), lambda i: (0, 0, i, 0)),
@@ -466,7 +459,7 @@
         compiler_params=pltpu.CompilerParams(vmem_limit_bytes=20 << 20),
         name="transform_y",
     )
-    return lambda spectrum, coupling: call(spectrum, jnp.asarray(y_high), jnp.asarray(y_low), coupling)
+    return lambda spectrum, coupling: call(spectrum, jnp.asarray(table), coupling)
 
 
 def per_device(multipoles, fractions, base_index, block_plane, atom_count, coupling):
@@ -476,7 +469,7 @@
     cells_y = NY // size_y
     block_count = block_plane.shape[0]
     devices = size_x * size_y
-    (x_high, x_low), _ = tables(size_x, size_y)
+    table, _ = tables(size_x, size_y)
     vmem = pltpu.VMEM
     whole = pl.BlockSpec(memory_space=pltpu.VMEM)
     limit = pltpu.CompilerParams(vmem_limit_bytes=20 << 20)
@@ -502,12 +495,12 @@
     spectrum = pl.pallas_call(
         lambda *refs: x_kernel(size_x, cells_x, *refs),
         out_shape=jax.ShapeDtypeStruct((devices * 32, LANES), F32),
-        in_specs=[whole] * 3,
+        in_specs=[whole] * 2,
         out_specs=whole,
-        scratch_shapes=[vmem((NX, 8 * LANES), F32), vmem((NX, 8 * LANES), BF16)],
+        scratch_shapes=[vmem((NX, 8 * LANES), BF16)],
         compiler_params=limit,
         name="transform_x",
-    )(density, jnp.asarray(x_high), jnp.asarray(x_low))
+    )(density, jnp.asarray(table))
 
     spectrum = lax.all_to_all(
         spectrum.reshape(devices, 32, LANES), ("gx", "gy"), split_axis=0, concat_axis=0, tiled=True

time: 103 us -> 103 us (level)
  blocking collectives: 73.2 us -> 74.6 us
  starting transfers between devices: 3.33 us -> 2.18 us
    all_to_all x1, blocking collectives: 39.5 us -> 40.9 us  [per_device(): lax.all_to_all(density, 'gx', split_axis=0, concat_axis=0, tiled=True)]
    ppermute x1, starting transfers between devices: 3.33 us -> 2.18 us  [per_device(): lax.ppermute(rim, 'gy', [(i, (i + 1) % size_y) for i in range(size_y)])]
where the time goes in v4:
time: 103 us
  blocking collectives  74.6 us (72%)
  Pallas kernels  21.9 us (21%)
  waiting for transfers between devices  3.94 us (4%)
  starting transfers between devices  2.18 us (2%)
    all_to_all x1, blocking collectives, per_device(): lax.all_to_all(density, 'gx', split_axis=0, concat_axis=0, tiled=True)  40.9 us
    all_to_all x1, blocking collectives, per_device(): lax.all_to_all(spectrum.reshape(devices, 32, LANES), ('gx', 'gy'), split_...  33.7 us
    pallas_call x1, Pallas kernels, per_device(): make_spread(block_count, cells_x, cells_y, size_x)  14.2 us
    ppermute x1, waiting for transfers between devices, per_device(): lax.ppermute(rim, 'gy', [(i, (i + 1) % size_y) for i in range(size_y)])  3.94 us
    pallas_call x1, Pallas kernels, make_y(): call(spectrum, jnp.asarray(table), coupling)  3.63 us
    pallas_call x1, Pallas kernels, per_device(): pl.pallas_call(lambda *refs: x_kernel(size_x, cells_x, *refs), out_shape=...  2.6 us
    ppermute x1, starting transfers between devices, per_device(): lax.ppermute(rim, 'gy', [(i, (i + 1) % size_y) for i in range(size_y)])  2.18 us
  transfers between devices with their start and end apart: 1, of which 1 were waited for; matrix products, arithmetic and copies ran while one was open for 0% of the time, Pallas kernels for 1%

profile of v4, /device:TPU:1, one launch (start us, length us, event | category | flops | bytes accessed | tf_op | source)
XLA Modules:
  0.0 102.7 jit_solution(15564338894394177596)
XLA Ops:
  0.0 14.2 %spread.1 = (f32[2,2240,128]{2,1,0:T(8,128)S(1)}, f32[280,128]{1,0:T(8,128)S(1)}) custom-call(s32[64]{0:T(128)} %refs_0_.1, s32[64]{0:T(128)} %refs_1_.3, f32[10,8192]{1,0:T(8,128)} %refs_2_.2, f32[3,8192]{1,0:T(4,128)} %refs_3_.1, s32[3,8192]{1,0:T(4,128)} %refs_4_.1), custom_call_target="tpu_custom_call" | custom-call | tf_op jit(solution)/shard_map/spread/pallas_call | solution.py:479
  14.2 2.2 %collective-permute-start = (f32[280,128]{1,0:T(8,128)S(1)}, f32[280,128]{1,0:T(8,128)S(1)}, u32[]{:S(2)}, u32[]{:S(2)}) collective-permute-start(f32[280,128]{1,0:T(8,128)S(1)} %get-tuple-element.20), channel_id=1, source_target_pairs={{0,1},{1,2},{2,3},{3,4},{4,5},{5,6},{6,7},{7,0},{8,9},{9,10},{10,1... | collective-permute-start | bytes 430088 | tf_op jit(solution)/shard_map/ppermute | solution.py:483
  16.4 1.5 %lines.1 = f32[16,280,128]{2,1,0:T(8,128)S(1)} custom-call(f32[2,2240,128]{2,1,0:T(8,128)S(1)} %get-tuple-element.19.density_ref), custom_call_target="tpu_custom_call" | custom-call | tf_op jit(solution)/shard_map/lines/pallas_call | solution.py:484
  17.8 3.9 %collective-permute-done = f32[280,128]{1,0:T(8,128)S(1)} collective-permute-done((f32[280,128]{1,0:T(8,128)S(1)}, f32[280,128]{1,0:T(8,128)S(1)}, u32[]{:S(2)}, u32[]{:S(2)}) %collective-permute-start) | collective-permute-done | bytes 143392 | tf_op jit(solution)/shard_map/ppermute | solution.py:483
  21.8 0.0 copy-start.2
  21.8 40.9 %all_to_all.10.refs_0_ = f32[16,280,128]{2,1,0:T(8,128)S(1)} all-to-all(f32[16,280,128]{2,1,0:T(8,128)S(1)} %fusion), channel_id=1, replica_groups=mesh['gx'=16,'gy'=8] {'gx'}, dimensions={0} | all-to-all | bytes 4587520 | tf_op jit(solution)/shard_map/all_to_all | solution.py:493
  62.7 0.0 copy-done.2
  62.7 2.6 %transform_x.1 = f32[4096,128]{1,0:T(8,128)S(1)} custom-call(f32[16,280,128]{2,1,0:T(8,128)S(1)} %all_to_all.10.refs_0_, bf16[1024,512]{1,0:T(8,128)(2,1)S(1)} %copy-done.2), custom_call_target="tpu_custom_call" | custom-call | tf_op jit(solution)/shard_map/transform_x/pallas_call | solution.py:495
  65.3 0.0 copy-start
  65.3 0.0 copy-start.1
  65.4 33.7 %all_to_all.11 = f32[128,32,128]{2,1,0:T(8,128)S(1)} all-to-all(f32[128,32,128]{2,1,0:T(8,128)S(1)} %bitcast.5), channel_id=1, replica_groups=mesh['gx'=16,'gy'=8] {'gx','gy'}, dimensions={0} | all-to-all | bytes 4194304 | tf_op jit(solution)/shard_map/all_to_all | solution.py:505
  99.1 0.0 copy-done
  99.1 0.0 copy-done.1
  99.1 3.6 %transform_y.1 = f32[2,2,512,256]{3,2,1,0:T(8,128)} custom-call(f32[4096,128]{1,0:T(8,128)S(1)} %bitcast.4, bf16[2,512,512]{2,1,0:T(8,128)(2,1)S(1)} %copy-done.1, f32[8,256,256]{2,1,0:T(8,128)S(1)} %copy-done), custom_call_target="tpu_custom_call" | custom-call | tf_op jit(solution)/shard_map/transform_y/pallas_call | solution.py:462
  (1 shorter events, 0.0 us)
Async XLA Ops:
  14.2 7.6 %collective-permute-start = (f32[280,128]{1,0:T(8,128)S(1)}, f32[280,128]{1,0:T(8,128)S(1)}, u32[]{:S(2)}, u32[]{:S(2)}) collective-permute-start(f32[280,128]{1,0:T(8,128)S(1)} %get-tuple-element.20), channel_id=1, source_target_pairs={{0,1},{1,2},{2,3},{3,4},{4,5},{5,6},{6,7},{7,0},{8,9},{9,10},{10,1... | collective-permute-start | bytes 430088 | tf_op jit(solution)/shard_map/ppermute | solution.py:483
  21.8 40.9 %copy-start.2 = (bf16[1024,512]{1,0:T(8,128)(2,1)S(1)}, bf16[1024,512]{1,0:T(8,128)(2,1)}, u32[]{:S(2)}) copy-start(bf16[1024,512]{1,0:T(8,128)(2,1)} %constant.31.clone.refs_1_) | copy-start | bytes 3145732
  65.3 33.7 %copy-start = (f32[8,256,256]{2,1,0:T(8,128)S(1)}, f32[8,256,256]{2,1,0:T(8,128)}, u32[]{:S(2)}) copy-start(f32[8,256,256]{2,1,0:T(8,128)} %refs_2_.3) | copy-start | bytes 6291460
  65.3 33.7 %copy-start.1 = (bf16[2,512,512]{2,1,0:T(8,128)(2,1)S(1)}, bf16[2,512,512]{2,1,0:T(8,128)(2,1)}, u32[]{:S(2)}) copy-start(bf16[2,512,512]{2,1,0:T(8,128)(2,1)} %constant.32.clone.refs_1_) | copy-start | bytes 3145732

commit v5 on v4

--- a/solution.py
+++ b/solution.py
@@ -403,7 +403,7 @@
 
 def make_spread(block_count, cells_x, cells_y, size_x):
     lines = cells_x + 3
-    groups = (block_count + 2) * (cells_x // XB) + 2
+    groups = (block_count + 2) * (cells_x // XB) + 3
     vmem = pltpu.VMEM
     slots = block_count * LANES
     whole = pl.BlockSpec(memory_space=pltpu.VMEM)
@@ -423,7 +423,7 @@
             vmem((3, slots), jnp.int32),
             pltpu.SemaphoreType.DMA((5,)),
             vmem((groups * TILE, LANES), F32),
-            vmem((256, LANES), F32),
+            vmem((256 + TILE, LANES), F32),
             vmem((ROWS, 6 * LANES), BF16),
             vmem((NZ, 6 * LANES), BF16),
             vmem((ROWS, 6 * LANES), BF16),

time: 103 us -> 103 us (level)
  waiting for transfers between devices: 3.94 us -> 5.92 us
  blocking collectives: 74.6 us -> 72.7 us
    ppermute x1, waiting for transfers between devices: 3.94 us -> 5.92 us  [per_device(): lax.ppermute(rim, 'gy', [(i, (i + 1) % size_y) for i in range(size_y)])]
    all_to_all x1, blocking collectives: 40.9 us -> 39 us  [per_device(): lax.all_to_all(density, 'gx', split_axis=0, concat_axis=0, tiled=True)]
where the time goes in v5:
time: 103 us
  blocking collectives  72.7 us (71%)
  Pallas kernels  22 us (21%)
  waiting for transfers between devices  5.92 us (6%)
  starting transfers between devices  2.05 us (2%)
    all_to_all x1, blocking collectives, per_device(): lax.all_to_all(density, 'gx', split_axis=0, concat_axis=0, tiled=True)  39 us
    all_to_all x1, blocking collectives, per_device(): lax.all_to_all(spectrum.reshape(devices, 32, LANES), ('gx', 'gy'), split_...  33.7 us
    pallas_call x1, Pallas kernels, per_device(): make_spread(block_count, cells_x, cells_y, size_x)  14.3 us
    ppermute x1, waiting for transfers between devices, per_device(): lax.ppermute(rim, 'gy', [(i, (i + 1) % size_y) for i in range(size_y)])  5.92 us
    pallas_call x1, Pallas kernels, make_y(): call(spectrum, jnp.asarray(table), coupling)  3.63 us
    pallas_call x1, Pallas kernels, per_device(): pl.pallas_call(lambda *refs: x_kernel(size_x, cells_x, *refs), out_shape=...  2.59 us
  transfers between devices with their start and end apart: 1, of which 1 were waited for; matrix products, arithmetic and copies ran while one was open for 0% of the time, Pallas kernels for 1%

profile of v5, /device:TPU:1, one launch (start us, length us, event | category | flops | bytes accessed | tf_op | source)
XLA Modules:
  0.0 102.8 jit_solution(16457317969130888175)
XLA Ops:
  0.0 14.3 %spread.1 = (f32[2,2240,128]{2,1,0:T(8,128)S(1)}, f32[280,128]{1,0:T(8,128)S(1)}) custom-call(s32[64]{0:T(128)} %refs_0_.1, s32[64]{0:T(128)} %refs_1_.3, f32[10,8192]{1,0:T(8,128)} %refs_2_.2, f32[3,8192]{1,0:T(4,128)} %refs_3_.1, s32[3,8192]{1,0:T(4,128)} %refs_4_.1), custom_call_target="tpu_custom_call" | custom-call | tf_op jit(solution)/shard_map/spread/pallas_call | solution.py:479
  14.3 2.1 %collective-permute-start = (f32[280,128]{1,0:T(8,128)S(1)}, f32[280,128]{1,0:T(8,128)S(1)}, u32[]{:S(2)}, u32[]{:S(2)}) collective-permute-start(f32[280,128]{1,0:T(8,128)S(1)} %get-tuple-element.20), channel_id=1, source_target_pairs={{0,1},{1,2},{2,3},{3,4},{4,5},{5,6},{6,7},{7,0},{8,9},{9,10},{10,1... | collective-permute-start | bytes 430088 | tf_op jit(solution)/shard_map/ppermute | solution.py:483
  16.4 1.5 %lines.1 = f32[16,280,128]{2,1,0:T(8,128)S(1)} custom-call(f32[2,2240,128]{2,1,0:T(8,128)S(1)} %get-tuple-element.19.density_ref), custom_call_target="tpu_custom_call" | custom-call | tf_op jit(solution)/shard_map/lines/pallas_call | solution.py:484
  17.9 5.9 %collective-permute-done = f32[280,128]{1,0:T(8,128)S(1)} collective-permute-done((f32[280,128]{1,0:T(8,128)S(1)}, f32[280,128]{1,0:T(8,128)S(1)}, u32[]{:S(2)}, u32[]{:S(2)}) %collective-permute-start) | collective-permute-done | bytes 143392 | tf_op jit(solution)/shard_map/ppermute | solution.py:483
  23.8 0.0 copy-start.2
  23.9 39.0 %all_to_all.10.refs_0_ = f32[16,280,128]{2,1,0:T(8,128)S(1)} all-to-all(f32[16,280,128]{2,1,0:T(8,128)S(1)} %fusion), channel_id=1, replica_groups=mesh['gx'=16,'gy'=8] {'gx'}, dimensions={0} | all-to-all | bytes 4587520 | tf_op jit(solution)/shard_map/all_to_all | solution.py:493
  62.8 0.0 copy-done.2
  62.8 2.6 %transform_x.1 = f32[4096,128]{1,0:T(8,128)S(1)} custom-call(f32[16,280,128]{2,1,0:T(8,128)S(1)} %all_to_all.10.refs_0_, bf16[1024,512]{1,0:T(8,128)(2,1)S(1)} %copy-done.2), custom_call_target="tpu_custom_call" | custom-call | tf_op jit(solution)/shard_map/transform_x/pallas_call | solution.py:495
  65.4 0.0 copy-start
  65.4 0.0 copy-start.1
  65.5 33.7 %all_to_all.11 = f32[128,32,128]{2,1,0:T(8,128)S(1)} all-to-all(f32[128,32,128]{2,1,0:T(8,128)S(1)} %bitcast.5), channel_id=1, replica_groups=mesh['gx'=16,'gy'=8] {'gx','gy'}, dimensions={0} | all-to-all | bytes 4194304 | tf_op jit(solution)/shard_map/all_to_all | solution.py:505
  99.2 0.0 copy-done
  99.2 0.0 copy-done.1
  99.2 3.6 %transform_y.1 = f32[2,2,512,256]{3,2,1,0:T(8,128)} custom-call(f32[4096,128]{1,0:T(8,128)S(1)} %bitcast.4, bf16[2,512,512]{2,1,0:T(8,128)(2,1)S(1)} %copy-done.1, f32[8,256,256]{2,1,0:T(8,128)S(1)} %copy-done), custom_call_target="tpu_custom_call" | custom-call | tf_op jit(solution)/shard_map/transform_y/pallas_call | solution.py:462
  (1 shorter events, 0.0 us)
Async XLA Ops:
  14.3 9.5 %collective-permute-start = (f32[280,128]{1,0:T(8,128)S(1)}, f32[280,128]{1,0:T(8,128)S(1)}, u32[]{:S(2)}, u32[]{:S(2)}) collective-permute-start(f32[280,128]{1,0:T(8,128)S(1)} %get-tuple-element.20), channel_id=1, source_target_pairs={{0,1},{1,2},{2,3},{3,4},{4,5},{5,6},{6,7},{7,0},{8,9},{9,10},{10,1... | collective-permute-start | bytes 430088 | tf_op jit(solution)/shard_map/ppermute | solution.py:483
  23.8 39.0 %copy-start.2 = (bf16[1024,512]{1,0:T(8,128)(2,1)S(1)}, bf16[1024,512]{1,0:T(8,128)(2,1)}, u32[]{:S(2)}) copy-start(bf16[1024,512]{1,0:T(8,128)(2,1)} %constant.31.clone.refs_1_) | copy-start | bytes 3145732
  65.4 33.7 %copy-start = (f32[8,256,256]{2,1,0:T(8,128)S(1)}, f32[8,256,256]{2,1,0:T(8,128)}, u32[]{:S(2)}) copy-start(f32[8,256,256]{2,1,0:T(8,128)} %refs_2_.3) | copy-start | bytes 6291460
  65.4 33.7 %copy-start.1 = (bf16[2,512,512]{2,1,0:T(8,128)(2,1)S(1)}, bf16[2,512,512]{2,1,0:T(8,128)(2,1)}, u32[]{:S(2)}) copy-start(bf16[2,512,512]{2,1,0:T(8,128)(2,1)} %constant.32.clone.refs_1_) | copy-start | bytes 3145732

commit v6 on v4

--- a/solution.py
+++ b/solution.py
@@ -341,38 +341,41 @@
             )
 
 
-def y_kernel(per_step, in_ref, table_ref, coupling_ref, out_ref, data, spectrum):
-    @pl.when(pl.program_id(0) == 0)
-    def _():
-        half_y = NY // 2
-        sums = []
-        for odd in range(2):
-            for q in range(4):
-                for half in range(2):
-                    value = in_ref[pl.ds(odd * 8 + q * 2 + half, half_y, stride=16), :]
-                    same = slice(q * NZ + half * LANES, q * NZ + (half + 1) * LANES)
-                    swap = slice((q ^ 1) * NZ + half * LANES, (q ^ 1) * NZ + (half + 1) * LANES)
-                    data[odd, 0:half_y, same] = value.astype(BF16)
-                    data[odd, half_y:NY, swap] = (value if q % 2 else -value).astype(BF16)
-            sums.append(split_dot(table_ref[odd], data[odd]))
-        even, odd = sums
-        spectrum[0:half_y, :] = (even + odd).astype(BF16)
-        spectrum[half_y:NY, :] = (even - odd).astype(BF16)
+def y_kernel(in_ref, table_ref, coupling_ref, out_ref, data, spectrum, ready, sent):
+    half_y = NY // 2
+    sums = []
+    for odd in range(2):
+        for q in range(4):
+            for half in range(2):
+                value = in_ref[pl.ds(odd * 8 + q * 2 + half, half_y, stride=16), :]
+                same = slice(q * NZ + half * LANES, q * NZ + (half + 1) * LANES)
+                swap = slice((q ^ 1) * NZ + half * LANES, (q ^ 1) * NZ + (half + 1) * LANES)
+                data[odd, 0:half_y, same] = value.astype(BF16)
+                data[odd, half_y:NY, swap] = (value if q % 2 else -value).astype(BF16)
+        sums.append(split_dot(table_ref[odd], data[odd]))
+    even, odd = sums
+    spectrum[0:half_y, :] = (even + odd).astype(BF16)
+    spectrum[half_y:NY, :] = (even - odd).astype(BF16)
 
     block = NY // MBLK
     dims = (((1,), (1,)), ((), ()))
-    for member in range(per_step):
-        first = (pl.program_id(0) * per_step + member) * block
-        rows = spectrum[pl.ds(pl.multiple_of(first, block), block), :]
+    copies = []
+    for b in range(MBLK):
+        rows = spectrum[b * block:(b + 1) * block, :]
         rows = jnp.concatenate([rows[:, q * NZ:(q + 1) * NZ] for q in range(4)], axis=0)
-        weight = coupling_ref[member]
+        weight = coupling_ref[b]
         high = weight.astype(BF16)
         low = (weight - high.astype(F32)).astype(BF16)
         result = lax.dot_general(rows, high, dims, preferred_element_type=F32) + lax.dot_general(
             rows, low, dims, preferred_element_type=F32
         )
         for q in range(4):
-            out_ref[q % 2, q // 2, member * block:(member + 1) * block, :] = result[q * block:(q + 1) * block]
+            ready[b, q % 2, q // 2, :, :] = result[q * block:(q + 1) * block]
+        copy = pltpu.make_async_copy(ready.at[b], out_ref.at[:, :, pl.ds(b * block, block), :], sent.at[b])
+        copy.start()
+        copies.append(copy)
+    for copy in copies:
+        copy.wait()
 
 
 def two_parts(table):
@@ -440,22 +443,20 @@
     )
 
 
-def make_y(size_x, size_y, per_step):
-    devices = size_x * size_y
+def make_y(size_x, size_y):
     _, table = tables(size_x, size_y)
     vmem = pltpu.VMEM
-    fixed = lambda i: (0, 0)
     call = pl.pallas_call(
-        lambda *refs: y_kernel(per_step, *refs),
+        y_kernel,
         out_shape=jax.ShapeDtypeStruct((2, 2, NY, NZ), F32),
-        grid=(MBLK // per_step,),
-        in_specs=[
-            pl.BlockSpec((devices * 32, LANES), fixed, pipeline_mode=pl.Buffered(1)),
-            pl.BlockSpec((2, NY, NY), lambda i: (0, 0, 0), pipeline_mode=pl.Buffered(1)),
-            pl.BlockSpec((per_step, NZ, NZ), lambda i: (i, 0, 0)),
+        in_specs=[pl.BlockSpec(memory_space=pltpu.VMEM)] * 3,
+        out_specs=pl.BlockSpec(memory_space=pltpu.MemorySpace.HBM),
+        scratch_shapes=[
+            vmem((2, NY, 4 * NZ), BF16),
+            vmem((NY, 4 * NZ), BF16),
+            vmem((MBLK, 2, 2, NY // MBLK, NZ), F32),
+            pltpu.SemaphoreType.DMA((MBLK,)),
         ],
-        out_specs=pl.BlockSpec((2, 2, NY // MBLK * per_step, NZ), lambda i: (0, 0, i, 0)),
-        scratch_shapes=[vmem((2, NY, 4 * NZ), BF16), vmem((NY, 4 * NZ), BF16)],
         compiler_params=pltpu.CompilerParams(vmem_limit_bytes=20 << 20),
         name="transform_y",
     )
@@ -506,7 +507,7 @@
         spectrum.reshape(devices, 32, LANES), ("gx", "gy"), split_axis=0, concat_axis=0, tiled=True
     ).reshape(devices * 32, LANES)
 
-    return make_y(size_x, size_y, 4)(spectrum, coupling)
+    return make_y(size_x, size_y)(spectrum, coupling)
 
 
 def solution(mesh):

time: 103 us -> 103 us (level)
  waiting for transfers between devices: 3.94 us -> 6.35 us
  blocking collectives: 74.6 us -> 72.2 us
    ppermute x1, waiting for transfers between devices: 3.94 us -> 6.35 us  [per_device(): lax.ppermute(rim, 'gy', [(i, (i + 1) % size_y) for i in range(size_y)])]
    all_to_all x1, blocking collectives: 40.9 us -> 38.5 us  [per_device(): lax.all_to_all(density, 'gx', split_axis=0, concat_axis=0, tiled=True)]
where the time goes in v6:
time: 103 us
  blocking collectives  72.2 us (70%)
  Pallas kernels  21.5 us (21%)
  waiting for transfers between devices  6.35 us (6%)
  starting transfers between devices  2.35 us (2%)
    all_to_all x1, blocking collectives, per_device(): lax.all_to_all(density, 'gx', split_axis=0, concat_axis=0, tiled=True)  38.5 us
    all_to_all x1, blocking collectives, per_device(): lax.all_to_all(spectrum.reshape(devices, 32, LANES), ('gx', 'gy'), split_...  33.7 us
    pallas_call x1, Pallas kernels, per_device(): make_spread(block_count, cells_x, cells_y, size_x)  14.2 us
    ppermute x1, waiting for transfers between devices, per_device(): lax.ppermute(rim, 'gy', [(i, (i + 1) % size_y) for i in range(size_y)])  6.35 us
    pallas_call x1, Pallas kernels, make_y(): call(spectrum, jnp.asarray(table), coupling)  3.24 us
    pallas_call x1, Pallas kernels, per_device(): pl.pallas_call(lambda *refs: x_kernel(size_x, cells_x, *refs), out_shape=...  2.59 us
    ppermute x1, starting transfers between devices, per_device(): lax.ppermute(rim, 'gy', [(i, (i + 1) % size_y) for i in range(size_y)])  2.35 us
  transfers between devices with their start and end apart: 1, of which 1 were waited for; matrix products, arithmetic and copies ran while one was open for 0% of the time, Pallas kernels for 1%

profile of v6, /device:TPU:1, one launch (start us, length us, event | category | flops | bytes accessed | tf_op | source)
XLA Modules:
  0.0 102.5 jit_solution(6744842020394399202)
XLA Ops:
  0.0 14.2 %spread.1 = (f32[2,2240,128]{2,1,0:T(8,128)S(1)}, f32[280,128]{1,0:T(8,128)S(1)}) custom-call(s32[64]{0:T(128)} %refs_0_.1, s32[64]{0:T(128)} %refs_1_.2, f32[10,8192]{1,0:T(8,128)} %refs_2_.1, f32[3,8192]{1,0:T(4,128)} %refs_3_.1, s32[3,8192]{1,0:T(4,128)} %refs_4_.1), custom_call_target="tpu_custom_call" | custom-call | tf_op jit(solution)/shard_map/spread/pallas_call | solution.py:480
  14.2 2.4 %collective-permute-start = (f32[280,128]{1,0:T(8,128)S(1)}, f32[280,128]{1,0:T(8,128)S(1)}, u32[]{:S(2)}, u32[]{:S(2)}) collective-permute-start(f32[280,128]{1,0:T(8,128)S(1)} %get-tuple-element.20), channel_id=1, source_target_pairs={{0,1},{1,2},{2,3},{3,4},{4,5},{5,6},{6,7},{7,0},{8,9},{9,10},{10,1... | collective-permute-start | bytes 430088 | tf_op jit(solution)/shard_map/ppermute | solution.py:484
  16.5 1.5 %lines.1 = f32[16,280,128]{2,1,0:T(8,128)S(1)} custom-call(f32[2,2240,128]{2,1,0:T(8,128)S(1)} %get-tuple-element.19.density_ref), custom_call_target="tpu_custom_call" | custom-call | tf_op jit(solution)/shard_map/lines/pallas_call | solution.py:485
  18.0 6.4 %collective-permute-done = f32[280,128]{1,0:T(8,128)S(1)} collective-permute-done((f32[280,128]{1,0:T(8,128)S(1)}, f32[280,128]{1,0:T(8,128)S(1)}, u32[]{:S(2)}, u32[]{:S(2)}) %collective-permute-start) | collective-permute-done | bytes 143392 | tf_op jit(solution)/shard_map/ppermute | solution.py:484
  24.4 0.0 copy-start.2
  24.4 38.5 %all_to_all.10.refs_0_ = f32[16,280,128]{2,1,0:T(8,128)S(1)} all-to-all(f32[16,280,128]{2,1,0:T(8,128)S(1)} %fusion), channel_id=1, replica_groups=mesh['gx'=16,'gy'=8] {'gx'}, dimensions={0} | all-to-all | bytes 4587520 | tf_op jit(solution)/shard_map/all_to_all | solution.py:494
  62.9 0.0 copy-done.2
  62.9 2.6 %transform_x.1 = f32[4096,128]{1,0:T(8,128)S(1)} custom-call(f32[16,280,128]{2,1,0:T(8,128)S(1)} %all_to_all.10.refs_0_, bf16[1024,512]{1,0:T(8,128)(2,1)S(1)} %copy-done.2), custom_call_target="tpu_custom_call" | custom-call | tf_op jit(solution)/shard_map/transform_x/pallas_call | solution.py:496
  65.5 0.0 copy-start
  65.5 0.0 copy-start.1
  65.6 33.7 %all_to_all.11 = f32[128,32,128]{2,1,0:T(8,128)S(1)} all-to-all(f32[128,32,128]{2,1,0:T(8,128)S(1)} %bitcast.5), channel_id=1, replica_groups=mesh['gx'=16,'gy'=8] {'gx','gy'}, dimensions={0} | all-to-all | bytes 4194304 | tf_op jit(solution)/shard_map/all_to_all | solution.py:506
  99.3 0.0 copy-done
  99.3 0.0 copy-done.1
  99.3 3.2 %transform_y.1 = f32[2,2,512,256]{3,2,1,0:T(8,128)} custom-call(f32[4096,128]{1,0:T(8,128)S(1)} %bitcast.4, bf16[2,512,512]{2,1,0:T(8,128)(2,1)S(1)} %copy-done.1, f32[8,256,256]{2,1,0:T(8,128)S(1)} %copy-done), custom_call_target="tpu_custom_call" | custom-call | tf_op jit(solution)/shard_map/transform_y/pallas_call | solution.py:463
  (1 shorter events, 0.0 us)
Async XLA Ops:
  14.2 10.2 %collective-permute-start = (f32[280,128]{1,0:T(8,128)S(1)}, f32[280,128]{1,0:T(8,128)S(1)}, u32[]{:S(2)}, u32[]{:S(2)}) collective-permute-start(f32[280,128]{1,0:T(8,128)S(1)} %get-tuple-element.20), channel_id=1, source_target_pairs={{0,1},{1,2},{2,3},{3,4},{4,5},{5,6},{6,7},{7,0},{8,9},{9,10},{10,1... | collective-permute-start | bytes 430088 | tf_op jit(solution)/shard_map/ppermute | solution.py:484
  24.4 38.5 %copy-start.2 = (bf16[1024,512]{1,0:T(8,128)(2,1)S(1)}, bf16[1024,512]{1,0:T(8,128)(2,1)}, u32[]{:S(2)}) copy-start(bf16[1024,512]{1,0:T(8,128)(2,1)} %constant.31.clone.refs_1_) | copy-start | bytes 3145732
  65.5 33.7 %copy-start = (f32[8,256,256]{2,1,0:T(8,128)S(1)}, f32[8,256,256]{2,1,0:T(8,128)}, u32[]{:S(2)}) copy-start(f32[8,256,256]{2,1,0:T(8,128)} %coupling_ref.1) | copy-start | bytes 6291460
  65.5 33.7 %copy-start.1 = (bf16[2,512,512]{2,1,0:T(8,128)(2,1)S(1)}, bf16[2,512,512]{2,1,0:T(8,128)(2,1)}, u32[]{:S(2)}) copy-start(bf16[2,512,512]{2,1,0:T(8,128)(2,1)} %constant.32.clone.table_ref) | copy-start | bytes 3145732

commit v7 on v6

--- a/solution.py
+++ b/solution.py
@@ -20,7 +20,7 @@
 ROWS_Y = 64
 WIN_X = XB + 3
 ROWS = WIN_X * ROWS_Y + 3 * TILE
-BATCH = 8
+BATCH = 16
 BUILD_STEPS = 3
 CHUNKS = ((0, 128), (128, 128), (256, 128), (384, 128), (512, 128), (640, 112))
 F32 = jnp.float32

time: 103 us -> 102 us (level)
  Pallas kernels: 21.5 us -> 20.3 us
    pallas_call x1, Pallas kernels: 14.2 us -> 13 us  [per_device(): make_spread(block_count, cells_x, cells_y, size_x)]
where the time goes in v7:
time: 102 us
  blocking collectives  71.6 us (70%)
  Pallas kernels  20.3 us (20%)
  waiting for transfers between devices  6.45 us (6%)
  starting transfers between devices  3.17 us (3%)
    all_to_all x1, blocking collectives, per_device(): lax.all_to_all(density, 'gx', split_axis=0, concat_axis=0, tiled=True)  37.8 us
    all_to_all x1, blocking collectives, per_device(): lax.all_to_all(spectrum.reshape(devices, 32, LANES), ('gx', 'gy'), split_...  33.8 us
    pallas_call x1, Pallas kernels, per_device(): make_spread(block_count, cells_x, cells_y, size_x)  13 us
    ppermute x1, waiting for transfers between devices, per_device(): lax.ppermute(rim, 'gy', [(i, (i + 1) % size_y) for i in range(size_y)])  6.45 us
    pallas_call x1, Pallas kernels, make_y(): call(spectrum, jnp.asarray(table), coupling)  3.24 us
    ppermute x1, starting transfers between devices, per_device(): lax.ppermute(rim, 'gy', [(i, (i + 1) % size_y) for i in range(size_y)])  3.17 us
    pallas_call x1, Pallas kernels, per_device(): pl.pallas_call(lambda *refs: x_kernel(size_x, cells_x, *refs), out_shape=...  2.6 us
  transfers between devices with their start and end apart: 1, of which 1 were waited for; matrix products, arithmetic and copies ran while one was open for 0% of the time, Pallas kernels for 1%

profile of v7, /device:TPU:1, one launch (start us, length us, event | category | flops | bytes accessed | tf_op | source)
XLA Modules:
  0.0 101.6 jit_solution(53973252262326251)
XLA Ops:
  0.0 13.0 %spread.1 = (f32[2,2240,128]{2,1,0:T(8,128)S(1)}, f32[280,128]{1,0:T(8,128)S(1)}) custom-call(s32[64]{0:T(128)} %refs_0_.1, s32[64]{0:T(128)} %refs_1_.2, f32[10,8192]{1,0:T(8,128)} %refs_2_.1, f32[3,8192]{1,0:T(4,128)} %refs_3_.1, s32[3,8192]{1,0:T(4,128)} %refs_4_.1), custom_call_target="tpu_custom_call" | custom-call | tf_op jit(solution)/shard_map/spread/pallas_call | solution.py:480
  13.0 3.2 %collective-permute-start = (f32[280,128]{1,0:T(8,128)S(1)}, f32[280,128]{1,0:T(8,128)S(1)}, u32[]{:S(2)}, u32[]{:S(2)}) collective-permute-start(f32[280,128]{1,0:T(8,128)S(1)} %get-tuple-element.20), channel_id=1, source_target_pairs={{0,1},{1,2},{2,3},{3,4},{4,5},{5,6},{6,7},{7,0},{8,9},{9,10},{10,1... | collective-permute-start | bytes 430088 | tf_op jit(solution)/shard_map/ppermute | solution.py:484
  16.2 1.5 %lines.1 = f32[16,280,128]{2,1,0:T(8,128)S(1)} custom-call(f32[2,2240,128]{2,1,0:T(8,128)S(1)} %get-tuple-element.19.density_ref), custom_call_target="tpu_custom_call" | custom-call | tf_op jit(solution)/shard_map/lines/pallas_call | solution.py:485
  17.7 6.5 %collective-permute-done = f32[280,128]{1,0:T(8,128)S(1)} collective-permute-done((f32[280,128]{1,0:T(8,128)S(1)}, f32[280,128]{1,0:T(8,128)S(1)}, u32[]{:S(2)}, u32[]{:S(2)}) %collective-permute-start) | collective-permute-done | bytes 143392 | tf_op jit(solution)/shard_map/ppermute | solution.py:484
  24.2 0.0 copy-start.2
  24.2 37.8 %all_to_all.10.refs_0_ = f32[16,280,128]{2,1,0:T(8,128)S(1)} all-to-all(f32[16,280,128]{2,1,0:T(8,128)S(1)} %fusion), channel_id=1, replica_groups=mesh['gx'=16,'gy'=8] {'gx'}, dimensions={0} | all-to-all | bytes 4587520 | tf_op jit(solution)/shard_map/all_to_all | solution.py:494
  61.9 0.0 copy-done.2
  61.9 2.6 %transform_x.1 = f32[4096,128]{1,0:T(8,128)S(1)} custom-call(f32[16,280,128]{2,1,0:T(8,128)S(1)} %all_to_all.10.refs_0_, bf16[1024,512]{1,0:T(8,128)(2,1)S(1)} %copy-done.2), custom_call_target="tpu_custom_call" | custom-call | tf_op jit(solution)/shard_map/transform_x/pallas_call | solution.py:496
  64.5 0.0 copy-start
  64.5 0.0 copy-start.1
  64.6 33.8 %all_to_all.11 = f32[128,32,128]{2,1,0:T(8,128)S(1)} all-to-all(f32[128,32,128]{2,1,0:T(8,128)S(1)} %bitcast.5), channel_id=1, replica_groups=mesh['gx'=16,'gy'=8] {'gx','gy'}, dimensions={0} | all-to-all | bytes 4194304 | tf_op jit(solution)/shard_map/all_to_all | solution.py:506
  98.4 0.0 copy-done
  98.4 0.0 copy-done.1
  98.4 3.2 %transform_y.1 = f32[2,2,512,256]{3,2,1,0:T(8,128)} custom-call(f32[4096,128]{1,0:T(8,128)S(1)} %bitcast.4, bf16[2,512,512]{2,1,0:T(8,128)(2,1)S(1)} %copy-done.1, f32[8,256,256]{2,1,0:T(8,128)S(1)} %copy-done), custom_call_target="tpu_custom_call" | custom-call | tf_op jit(solution)/shard_map/transform_y/pallas_call | solution.py:463
  (1 shorter events, 0.0 us)
Async XLA Ops:
  13.0 11.1 %collective-permute-start = (f32[280,128]{1,0:T(8,128)S(1)}, f32[280,128]{1,0:T(8,128)S(1)}, u32[]{:S(2)}, u32[]{:S(2)}) collective-permute-start(f32[280,128]{1,0:T(8,128)S(1)} %get-tuple-element.20), channel_id=1, source_target_pairs={{0,1},{1,2},{2,3},{3,4},{4,5},{5,6},{6,7},{7,0},{8,9},{9,10},{10,1... | collective-permute-start | bytes 430088 | tf_op jit(solution)/shard_map/ppermute | solution.py:484
  24.2 37.8 %copy-start.2 = (bf16[1024,512]{1,0:T(8,128)(2,1)S(1)}, bf16[1024,512]{1,0:T(8,128)(2,1)}, u32[]{:S(2)}) copy-start(bf16[1024,512]{1,0:T(8,128)(2,1)} %constant.31.clone.refs_1_) | copy-start | bytes 3145732
  64.5 33.8 %copy-start = (f32[8,256,256]{2,1,0:T(8,128)S(1)}, f32[8,256,256]{2,1,0:T(8,128)}, u32[]{:S(2)}) copy-start(f32[8,256,256]{2,1,0:T(8,128)} %coupling_ref.1) | copy-start | bytes 6291460
  64.5 33.8 %copy-start.1 = (bf16[2,512,512]{2,1,0:T(8,128)(2,1)S(1)}, bf16[2,512,512]{2,1,0:T(8,128)(2,1)}, u32[]{:S(2)}) copy-start(bf16[2,512,512]{2,1,0:T(8,128)(2,1)} %constant.32.clone.table_ref) | copy-start | bytes 3145732
